TPU v7x, 128 devices: a whole 4x4x4 slice. The times are simulated.
128 devices in a mesh: grp: 4 (over y), row: 32 (over x, z, core).
Axes of the slice: x: 4, y: 4, z: 4, core: 2. Of those that a mesh axis runs over, the one named last changes fastest.
Arguments:
- site_blocks: float32 [32, 4, 512, 256], P('grp', None, 'row'), may hold values from -40 to 40
- row_lengths: int32 [32], replicated, may hold values from 1 to 512, 8192 in all
- column_lengths: int32 [32], replicated, may hold values from 1 to 256, 4096 in all
- joining: int32 [32, 4], replicated, may hold values from 0 to 31, as said below
- owner_slots: int32 [32], replicated, may hold values from 0 to 31, each once
- next_blocks: float32 [32, 1024, 256], P('grp', 'row'), may hold values from -90 to 90
Outputs:
- canonical: float32 [32, 4, 512, 256], P('grp', None, 'row')
- next_site: float32 [32, 1024, 256], P('grp', 'row')
Inputs may be any that keep to these rules, and one draw needn't show every extreme that they name: `joining`: for each physical state, every joined sector is named by exactly one left sector. `owner_slots`: each joined sector is held in exactly one slot. `row_lengths`: one left sector has all 512 rows live.
All inputs are finite; a program needn't handle non-finite values.
Results may differ from a plain program's by a relative error of at most 0.00009.
Values sent between devices are 32-bit elements; how exact they have to be, the bound alone decides.
No kernel may reach another device: no remote copies, remote signals or barrier semaphores. Data moves between devices by JAX's collectives and lax.ppermute only.
A program may use at most 128 MiB of HBM per device.

v0:
```python
import math

import jax
import jax.numpy as jnp
from jax import lax
from jax.sharding import PartitionSpec as P

PRECISE = lax.Precision.HIGHEST


def leaf_factor(matrix):
    size = matrix.shape[-1]
    row_ids = jnp.arange(size, dtype=jnp.int32)

    def cholesky_step(column, state):
        lower, work = state
        select = (row_ids == column).astype(jnp.float32)
        current = jnp.sum(work * select[None, None, :], axis=-1)
        pivot = jnp.sqrt(jnp.sum(current * select[None, :], axis=-1, keepdims=True))
        current = jnp.where(row_ids[None, :] >= column, current / pivot, 0.0)
        lower = lower + current[:, :, None] * select[None, None, :]
        work = work - current[:, :, None] * current[:, None, :]
        return (lower, work)

    lower, unused = lax.fori_loop(0, size, cholesky_step, (jnp.zeros_like(matrix), matrix))

    def solve_step(position, inverse):
        select = (row_ids == position).astype(jnp.float32)
        lower_row = jnp.sum(lower * select[None, :, None], axis=1)
        pivot = jnp.sum(lower_row * select[None, :], axis=-1, keepdims=True)
        combined = jnp.einsum("bj,bjk->bk", lower_row, inverse, precision=PRECISE)
        fresh = (select[None, :] - combined) / pivot
        return inverse + select[None, :, None] * fresh[:, None, :]

    inverse = lax.fori_loop(0, size, solve_step, jnp.zeros_like(matrix))
    return (lower, inverse)


def lower_factor(matrix):
    size = matrix.shape[-1]
    if size <= 32 or size % 2 == 1:
        return leaf_factor(matrix)
    middle = size // 2
    top_left = matrix[..., :middle, :middle]
    bottom_left = matrix[..., middle:, :middle]
    bottom_right = matrix[..., middle:, middle:]
    first_lower, first_inverse = lower_factor(top_left)
    coupling = jnp.einsum("bij,bkj->bik", bottom_left, first_inverse, precision=PRECISE)
    reduced = bottom_right - jnp.einsum("bij,bkj->bik", coupling, coupling, precision=PRECISE)
    second_lower, second_inverse = lower_factor(reduced)
    cross = -jnp.einsum(
        "bij,bjk->bik",
        second_inverse,
        jnp.einsum("bij,bjk->bik", coupling, first_inverse, precision=PRECISE),
        precision=PRECISE,
    )
    zeros_block = jnp.zeros_like(bottom_left.swapaxes(-1, -2))
    lower = jnp.concatenate(
        [
            jnp.concatenate([first_lower, zeros_block], axis=-1),
            jnp.concatenate([coupling, second_lower], axis=-1),
        ],
        axis=-2,
    )
    inverse = jnp.concatenate(
        [
            jnp.concatenate([first_inverse, zeros_block], axis=-1),
            jnp.concatenate([cross, second_inverse], axis=-1),
        ],
        axis=-2,
    )
    return (lower, inverse)


def factor(gram_total, live_count, columns, identity):
    dead_cols = (columns[None, :] >= live_count[:, None]).astype(jnp.float32)
    gram_total = gram_total + dead_cols[:, :, None] * identity[None]
    lower, lower_inverse = lower_factor(gram_total)
    return (jnp.swapaxes(lower, 1, 2), jnp.swapaxes(lower_inverse, 1, 2))


def body(site_blocks, row_lengths, column_lengths, joining, owner_slots, next_blocks):
    sector_count, states, row_count, breadth = site_blocks.shape
    sector_total = row_lengths.shape[0]
    sectors = jnp.arange(sector_total, dtype=jnp.int32)
    columns = jnp.arange(breadth, dtype=jnp.int32)
    identity = jnp.eye(breadth, dtype=jnp.float32)
    n_row = lax.axis_size("row")
    first_sector = lax.axis_index("grp") * sector_count
    joined_hot = joining[:, :, None] == sectors[None, None, :]
    joined_rows = jnp.sum(jnp.where(joined_hot, row_lengths[:, None, None], 0), axis=(0, 1))
    live_cols = jnp.minimum(column_lengths, joined_rows // 2)
    local_join = lax.dynamic_slice_in_dim(joining, first_sector, sector_count, 0)
    local_rows = lax.dynamic_slice_in_dim(row_lengths, first_sector, sector_count, 0)
    local_owner = lax.dynamic_slice_in_dim(owner_slots, first_sector, sector_count, 0)
    local_hot = local_join[:, :, None] == sectors[None, None, :]
    piece_cols = jnp.sum(jnp.where(local_hot, live_cols[None, None, :], 0), axis=2)
    row_ids = lax.axis_index("row") * row_count + jnp.arange(row_count, dtype=jnp.int32)
    row_mask = (row_ids[None, :] < local_rows[:, None]).astype(jnp.float32)
    col_mask = (columns[None, None, :] < piece_cols[:, :, None]).astype(jnp.float32)
    masked = site_blocks * row_mask[:, None, :, None] * col_mask[:, :, None, :]
    hot_float = local_hot.astype(jnp.float32)
    full_scale = math.sqrt(states * row_count * n_row)
    pieces = jnp.einsum("psrk,psrl->pskl", masked, masked, precision=PRECISE)
    gram_sheet = jnp.einsum("psq,pskl->qkl", hot_float, pieces, precision=PRECISE)
    gram_total = lax.psum(gram_sheet, ("grp", "row"))
    upper_factor, inverse = factor(gram_total, live_cols, columns, identity)
    inverse_picked = jnp.einsum("psq,qkl->pskl", hot_float, inverse, precision=PRECISE)
    canonical = full_scale * jnp.einsum(
        "psrk,pskl->psrl", masked, inverse_picked, precision=PRECISE
    )
    owner_hot = (local_owner[:, None] == sectors[None, :]).astype(jnp.float32)
    upper_picked = jnp.einsum("pq,qkl->pkl", owner_hot, upper_factor, precision=PRECISE)
    slot_live = jnp.sum(
        jnp.where(local_owner[:, None] == sectors[None, :], live_cols[None, :], 0), axis=1
    )
    next_mask = (columns[None, :] < slot_live[:, None]).astype(jnp.float32)
    masked_next = next_blocks * next_mask[:, None, :]
    absorbed = jnp.einsum("pcj,pkj->pck", masked_next, upper_picked, precision=PRECISE)
    squares = lax.psum(jnp.sum(absorbed * absorbed), ("grp", "row"))
    entries = float(sector_total * next_blocks.shape[1] * n_row * breadth)
    next_site = absorbed * lax.rsqrt(squares / entries + 1e-06)
    return (canonical, next_site)


def solution(mesh):
    in_specs = (P("grp", None, "row", None), P(), P(), P(), P(), P("grp", "row", None))
    out_specs = (P("grp", None, "row", None), P("grp", "row", None))
    return jax.shard_map(body, mesh=mesh, in_specs=in_specs, out_specs=out_specs, check_vma=False)
```

profile of v0, /device:TPU:1, one launch (start us, length us, event | category | flops | bytes accessed | tf_op | source)
XLA Modules:
  0.0 1442.0 jit_solution(182005583636064985)
XLA Ops:
  10.7 8.3 fusion.137
  18.9 10.3 fusion.88
  31.2 162.7 %all-reduce.16.cloned.1.call-done = f32[32,256,256]{2,0,1:T(8,128)} async-done(((f32[32,256,256]{2,0,1:T(8,128)}), f32[32,256,256]{2,0,1:T(8,128)}) %all-reduce.16.cloned.1.call-update) | async-done | bytes 8388624 | tf_op jit(solution)/shard_map/psum | solution.py:106
  193.9 5.1 multiply_add_fusion.8
  204.3 123.9 %while.256 = (s32[]{:T(128)}, f32[32,32,32]{2,1,0:T(8,128)}, f32[32,32,32]{2,1,0:T(8,128)}, s32[]{:T(128)}, s32[]{:T(128)}) while((s32[]{:T(128)}, f32[32,32,32]{2,1,0:T(8,128)}, f32[32,32,32]{2,1,0:T(8,128)}, s32[]{:T(128)}, s32[]{:T(128)}) %tuple.542), condition=%wide.region_6.7_spmd.clone.clone, body=%wide.region_3.6_spmd.clone.clone.sunk | while | flops 232515 | bytes 677003 | solution.py:25
  328.2 67.4 %while.248 = (s32[]{:T(128)}, f32[32,32,32]{2,1,0:T(8,128)S(1)}, f32[32,32,32]{2,1,0:T(8,128)}, s32[]{:T(128)}, s32[]{:T(128)}) while((s32[]{:T(128)}, f32[32,32,32]{2,1,0:T(8,128)S(1)}, f32[32,32,32]{2,1,0:T(8,128)}, s32[]{:T(128)}, s32[]{:T(128)}) %tuple.545), condition=%wide.region_10.11_spmd.clone, body=%wide.region_7.10_spmd.clone.sunk | while | flops 592931 | bytes 553932 | solution.py:35
  405.2 124.7 %while.257 = (s32[]{:T(128)}, f32[32,32,32]{2,1,0:T(8,128)}, f32[32,32,32]{2,1,0:T(8,128)}, s32[]{:T(128)}, s32[]{:T(128)}) while((s32[]{:T(128)}, f32[32,32,32]{2,1,0:T(8,128)}, f32[32,32,32]{2,1,0:T(8,128)}, s32[]{:T(128)}, s32[]{:T(128)}) %tuple.548), condition=%wide.region_14.15_spmd.clone.clone, body=%wide.region_11.14_spmd.clone.clone.sunk | while | flops 232515 | bytes 677003 | solution.py:25
  532.6 156.6 %while.249 = (s32[]{:T(128)}, f32[32,32,32]{2,1,0:T(8,128)}, f32[32,32,32]{2,1,0:T(8,128)}, s32[]{:T(128)}, s32[]{:T(128)}) while((s32[]{:T(128)}, f32[32,32,32]{2,1,0:T(8,128)}, f32[32,32,32]{2,1,0:T(8,128)}, s32[]{:T(128)}, s32[]{:T(128)}) %tuple.551), condition=%wide.region_18.19_spmd.clone, body=%wide.region_15.18_spmd.clone.sunk | while | flops 592931 | bytes 553932 | solution.py:35
  702.1 84.4 %while.258 = (s32[]{:T(128)}, f32[32,32,32]{2,1,0:T(8,128)}, f32[32,32,32]{2,1,0:T(8,128)S(1)}, s32[]{:T(128)}, s32[]{:T(128)}) while((s32[]{:T(128)}, f32[32,32,32]{2,1,0:T(8,128)}, f32[32,32,32]{2,1,0:T(8,128)S(1)}, s32[]{:T(128)}, s32[]{:T(128)}) %tuple.554), condition=%wide.region_22.23_spmd.clone.clone, body=%wide.region_19.22_spmd.clone.clone.sunk | while | flops 232515 | bytes 677003 | solution.py:25
  786.5 67.4 %while.250 = (s32[]{:T(128)}, f32[32,32,32]{2,1,0:T(8,128)S(1)}, f32[32,32,32]{2,1,0:T(8,128)}, s32[]{:T(128)}, s32[]{:T(128)}) while((s32[]{:T(128)}, f32[32,32,32]{2,1,0:T(8,128)S(1)}, f32[32,32,32]{2,1,0:T(8,128)}, s32[]{:T(128)}, s32[]{:T(128)}) %tuple.557), condition=%wide.region_26.27_spmd.clone, body=%wide.region_23.26_spmd.clone.sunk | while | flops 592931 | bytes 553932 | solution.py:35
  861.6 85.0 %while.259 = (s32[]{:T(128)}, f32[32,32,32]{2,1,0:T(8,128)}, f32[32,32,32]{2,1,0:T(8,128)S(1)}, s32[]{:T(128)}, s32[]{:T(128)}) while((s32[]{:T(128)}, f32[32,32,32]{2,1,0:T(8,128)}, f32[32,32,32]{2,1,0:T(8,128)S(1)}, s32[]{:T(128)}, s32[]{:T(128)}) %tuple.560), condition=%wide.region_30.31_spmd.clone.clone, body=%wide.region_27.30_spmd.clone.clone.sunk | while | flops 232515 | bytes 677003 | solution.py:25
  946.6 67.4 %while.251 = (s32[]{:T(128)}, f32[32,32,32]{2,1,0:T(8,128)S(1)}, f32[32,32,32]{2,1,0:T(8,128)}, s32[]{:T(128)}, s32[]{:T(128)}) while((s32[]{:T(128)}, f32[32,32,32]{2,1,0:T(8,128)S(1)}, f32[32,32,32]{2,1,0:T(8,128)}, s32[]{:T(128)}, s32[]{:T(128)}) %tuple.563), condition=%wide.region_34.35_spmd.clone, body=%wide.region_31.34_spmd.clone.sunk | while | flops 592931 | bytes 553932 | solution.py:35
  1018.2 5.4 fusion.105
  1023.7 4.5 fusion.172
  1032.7 25.6 %while.260 = (s32[]{:T(128)}, f32[32,32,32]{2,1,0:T(8,128)S(1)}, f32[32,32,32]{2,1,0:T(8,128)S(1)}, s32[]{:T(128)}, s32[]{:T(128)}) while((s32[]{:T(128)}, f32[32,32,32]{2,1,0:T(8,128)S(1)}, f32[32,32,32]{2,1,0:T(8,128)S(1)}, s32[]{:T(128)}, s32[]{:T(128)}) %tuple.596), condition=%wide.region_38.39_spmd.clone.clone, body=%wide.region_35.38_spmd.clone.clone.sunk | while | flops 232515 | bytes 677003 | solution.py:25
  1058.3 34.1 %while.252 = (s32[]{:T(128)}, f32[32,32,32]{2,1,0:T(8,128)S(1)}, f32[32,32,32]{2,1,0:T(8,128)S(1)}, s32[]{:T(128)}, s32[]{:T(128)}) while((s32[]{:T(128)}, f32[32,32,32]{2,1,0:T(8,128)S(1)}, f32[32,32,32]{2,1,0:T(8,128)S(1)}, s32[]{:T(128)}, s32[]{:T(128)}) %tuple.569), condition=%wide.region_42.43_spmd.clone, body=%wide.region_39.42_spmd.clone.sunk | while | flops 592931 | bytes 553932 | solution.py:35
  1097.2 4.9 fusion.179
  1103.1 25.4 %while.261 = (s32[]{:T(128)}, f32[32,32,32]{2,1,0:T(8,128)S(1)}, f32[32,32,32]{2,1,0:T(8,128)S(1)}, s32[]{:T(128)}, s32[]{:T(128)}) while((s32[]{:T(128)}, f32[32,32,32]{2,1,0:T(8,128)S(1)}, f32[32,32,32]{2,1,0:T(8,128)S(1)}, s32[]{:T(128)}, s32[]{:T(128)}) %tuple.595), condition=%wide.region_46.47_spmd.clone.clone, body=%wide.region_43.46_spmd.clone.clone.sunk | while | flops 232515 | bytes 677003 | solution.py:25
  1130.8 34.4 %while.253 = (s32[]{:T(128)}, f32[32,32,32]{2,1,0:T(8,128)S(1)}, f32[32,32,32]{2,1,0:T(8,128)S(1)}, s32[]{:T(128)}, s32[]{:T(128)}) while((s32[]{:T(128)}, f32[32,32,32]{2,1,0:T(8,128)S(1)}, f32[32,32,32]{2,1,0:T(8,128)S(1)}, s32[]{:T(128)}, s32[]{:T(128)}) %tuple.592), condition=%wide.region_50.51_spmd.clone, body=%wide.region_47.50_spmd.clone.sunk | while | flops 592931 | bytes 553932 | solution.py:35
  1175.8 25.4 %while.262 = (s32[]{:T(128)}, f32[32,32,32]{2,1,0:T(8,128)S(1)}, f32[32,32,32]{2,1,0:T(8,128)S(1)}, s32[]{:T(128)}, s32[]{:T(128)}) while((s32[]{:T(128)}, f32[32,32,32]{2,1,0:T(8,128)S(1)}, f32[32,32,32]{2,1,0:T(8,128)S(1)}, s32[]{:T(128)}, s32[]{:T(128)}) %tuple.594), condition=%wide.region_54.55_spmd.clone.clone, body=%wide.region_51.54_spmd.clone.clone.sunk | while | flops 232515 | bytes 677003 | solution.py:25
  1201.2 34.2 %while.254 = (s32[]{:T(128)}, f32[32,32,32]{2,1,0:T(8,128)S(1)}, f32[32,32,32]{2,1,0:T(8,128)S(1)}, s32[]{:T(128)}, s32[]{:T(128)}) while((s32[]{:T(128)}, f32[32,32,32]{2,1,0:T(8,128)S(1)}, f32[32,32,32]{2,1,0:T(8,128)S(1)}, s32[]{:T(128)}, s32[]{:T(128)}) %tuple.581), condition=%wide.region_58.59_spmd.clone, body=%wide.region_55.58_spmd.clone.sunk | while | flops 592931 | bytes 553932 | solution.py:35
  1245.1 25.4 %while.263 = (s32[]{:T(128)}, f32[32,32,32]{2,1,0:T(8,128)S(1)}, f32[32,32,32]{2,1,0:T(8,128)S(1)}, s32[]{:T(128)}, s32[]{:T(128)}) while((s32[]{:T(128)}, f32[32,32,32]{2,1,0:T(8,128)S(1)}, f32[32,32,32]{2,1,0:T(8,128)S(1)}, s32[]{:T(128)}, s32[]{:T(128)}) %tuple.593), condition=%wide.region_62.63_spmd.clone.clone, body=%wide.region_59.62_spmd.clone.clone.sunk | while | flops 232515 | bytes 677003 | solution.py:25
  1270.5 7.4 fusion.76
  1277.9 10.3 copy.93
  1288.2 5.3 fusion.155
  1296.5 64.5 %psum.15 = f32[]{:T(128)} all-reduce(f32[]{:T(128)} %get-tuple-element.1834), channel_id=1, replica_groups=mesh['grp'=4,'row'=32] {'grp','row'}, use_global_device_ids=true, to_apply=%region_69.70 | all-reduce | flops 1 | bytes 8 | tf_op jit(solution)/shard_map/psum | solution.py:120
  1361.7 34.0 %while.255 = (s32[]{:T(128)}, f32[32,32,32]{2,1,0:T(8,128)S(1)}, f32[32,32,32]{2,1,0:T(8,128)S(1)}, s32[]{:T(128)}, s32[]{:T(128)}) while((s32[]{:T(128)}, f32[32,32,32]{2,1,0:T(8,128)S(1)}, f32[32,32,32]{2,1,0:T(8,128)S(1)}, s32[]{:T(128)}, s32[]{:T(128)}) %tuple.587), condition=%wide.region_66.67_spmd.clone, body=%wide.region_63.66_spmd.clone.sunk | while | flops 592931 | bytes 553932 | solution.py:35
  1398.9 4.6 fusion.109
  1403.5 5.7 fusion.77
  1409.2 10.3 copy.90
  1419.5 7.1 fusion.78
  1426.7 7.5 fusion.112
  (3263 shorter events, 1083.6 us)
Async XLA Ops:
  7.2 186.7 %all-reduce.16.cloned.1.call-start = ((), (), s32[]{:S(2)}) async-start(), calls=%async_computation | async-start | bytes 16777216 | tf_op jit(solution)/shard_map/psum | solution.py:106
  10.2 19.8 %copy-start.47 = (s32[32]{0:T(128)}, s32[32]{0:T(128)S(1)}, u32[]{:S(2)}) copy-start(s32[32]{0:T(128)S(1)} %fusion.158) | copy-start | bytes 388
  10.5 8.4 copy-start.44
  199.1 3.2 copy-start.12
  689.2 3.2 copy-start.38
  692.4 4.2 copy-start.17
  694.7 4.0 copy-start.13
  786.5 67.4 %copy-start.43 = (f32[32,32,32]{2,0,1:T(8,128)S(1)}, f32[32,32,32]{2,0,1:T(8,128)}, u32[]{:S(2)}) copy-start(f32[32,32,32]{2,0,1:T(8,128)} %get-tuple-element.1832) | copy-start | bytes 393220
  857.6 3.2 copy-start.34
  946.6 67.5 %copy-start.42 = (f32[32,32,32]{2,1,0:T(8,128)S(1)}, f32[32,32,32]{2,1,0:T(8,128)}, u32[]{:S(2)}) copy-start(f32[32,32,32]{2,1,0:T(8,128)} %fusion.170) | copy-start | bytes 393220
  1018.2 5.5 copy-start.9
  1023.7 4.5 copy-start.7
  1092.4 3.7 copy-start.20
  1093.7 3.5 copy-start.10
  1094.6 2.5 copy-start.8
  1128.5 2.3 copy-start
  1167.3 4.1 copy-start.15
  1171.4 2.2 copy-start.21
  1237.7 3.3 copy-start.22
  1237.7 3.3 copy-start.16
  1238.7 3.5 copy-start.5
  1238.7 3.5 copy-start.6
  1238.7 3.5 copy-start.14
  1238.7 3.5 copy-start.26
  1238.7 3.5 copy-start.39
  1277.9 10.3 copy-start.49
  1288.2 5.3 copy-start.46
  1361.7 34.1 %copy-start.41 = (f32[32,32,32]{2,1,0:T(8,128)S(1)}, f32[32,32,32]{2,1,0:T(8,128)}, u32[]{:S(2)}) copy-start(f32[32,32,32]{2,1,0:T(8,128)} %fusion.177) | copy-start | bytes 393220
  1361.7 34.7 %copy-start.30 = (f32[32,32,64]{2,1,0:T(8,128)S(1)}, f32[32,32,64]{2,1,0:T(8,128)}, u32[]{:S(2)}) copy-start(f32[32,32,64]{2,1,0:T(8,128)} %concatenate.140) | copy-start | bytes 786436
  1398.9 4.6 copy-start.11
  1419.5 7.1 copy-start.40
  1419.5 7.1 copy-start.45
  (20 other events, 25.5 us)
Sparse Core Ops, SparseCore 0:
  29.4 164.4 all-reduce.15
where the time goes:
time: 1470 us; the launch traced here: 1440 us
  other arithmetic  862 us (59%)
  matrix products  269 us (18%)
  waiting for transfers between devices  163 us (11%)
  blocking collectives  64.5 us (4%)
  local copies, waits for them, and re-layouts  49.2 us (3%)
  loops' own time  18.5 us (1%)
  between operations  16 us (1%)
    sub x256, other arithmetic, cholesky_step(): work = work - current[:, :, None] * current[:, None, :]  341 us
    reduce_sum x256, other arithmetic, solve_step(): lower_row = jnp.sum(lower * select[None, :, None], axis=1)  171 us
    dot_general x256, matrix products, solve_step(): combined = jnp.einsum('bj,bjk->bk', lower_row, inverse, precision=PRECISE)  171 us
    psum x1, waiting for transfers between devices, body(): gram_total = lax.psum(gram_sheet, ('grp', 'row'))  163 us
    reduce_sum x256, other arithmetic, cholesky_step(): current = jnp.sum(work * select[None, None, :], axis=-1)  120 us
    add x256, other arithmetic, solve_step(): return inverse + select[None, :, None] * fresh[:, None, :]  92.6 us
    psum x1, blocking collectives, body(): squares = lax.psum(jnp.sum(absorbed * absorbed), ('grp', 'row'))  64.5 us
  transfers between devices with their start and end apart: 1, of which 1 were waited for; matrix products, arithmetic and copies ran while one was open for 0% of the time, Pallas kernels for 0%

commit v1 on v0

v1 whole, which is shorter than its diff:
```python
import functools
import math

import jax
import jax.numpy as jnp
from jax import lax
from jax.experimental import pallas as pl
from jax.experimental.pallas import tpu as pltpu
from jax.sharding import PartitionSpec as P

PRECISE = lax.Precision.HIGHEST
HALF = 128
STEP = 8
SLOT = 8
HBM = pl.BlockSpec(memory_space=pltpu.HBM)
PARAMS = pltpu.CompilerParams(vmem_limit_bytes=16 * 1024 * 1024)
VMEM = pl.BlockSpec(memory_space=pltpu.VMEM)
SMEM = pl.BlockSpec(memory_space=pltpu.SMEM)


def dot(a, b, ca, cb):
    return lax.dot_general(
        a, b, (((ca,), (cb,)), ((), ())), precision=PRECISE, preferred_element_type=jnp.float32
    )


def live_count(join_row, rows_row, column_lengths, sector):
    joined = jnp.where(join_row[...] == sector, rows_row[...], 0.0)
    joined = jnp.sum(joined, axis=1, keepdims=True)
    return jnp.minimum(jnp.floor(joined * 0.5), column_lengths[sector].astype(jnp.float32))


def gather_kernel(site_ref, next_ref, out_ref, sems):
    here = site_ref.shape[1]
    one = pltpu.make_async_copy(site_ref, out_ref.at[:, :here, :], sems.at[0])
    two = pltpu.make_async_copy(next_ref, out_ref.at[:, here:, :], sems.at[1])
    one.start()
    two.start()
    one.wait()
    two.wait()


def scatter_kernel(data_ref, site_ref, next_ref, sems):
    here = site_ref.shape[1]
    one = pltpu.make_async_copy(data_ref.at[:, :here, :], site_ref, sems.at[0])
    two = pltpu.make_async_copy(data_ref.at[:, here:, :], next_ref, sems.at[1])
    one.start()
    two.start()
    one.wait()
    two.wait()


def slot_rows(index):
    return pl.ds(index, HALF, stride=SLOT)


def gram_kernel(meta, column_lengths, join_row, rows_row, unused_one, unused_two, data_ref, out_ref):
    peers, depth, breadth = data_ref.shape
    here = depth - STEP
    site = data_ref[:, :here, :].reshape(peers * here, breadth)
    row_ids = lax.broadcasted_iota(jnp.int32, site.shape, 0)
    site = jnp.where(row_ids < meta[0], site, 0.0)
    nxt = data_ref[:, here:, :].reshape(peers * STEP, breadth)
    live_slot = live_count(join_row, rows_row, column_lengths, meta[2])
    column_ids = lax.broadcasted_iota(jnp.int32, (1, breadth), 1).astype(jnp.float32)
    nxt = jnp.where(column_ids < live_slot, nxt, 0.0)
    for start, block in ((0, site), (3, nxt)):
        top = dot(block[:, :HALF], block, 0, 0)
        out_ref[slot_rows(start), :] = top[:, :HALF]
        out_ref[slot_rows(start + 1), :] = top[:, HALF:]
        out_ref[slot_rows(start + 2), :] = dot(block[:, HALF:], block[:, HALF:], 0, 0)


def combine_kernel(join_row, join_col, owner_col, piece_ref, out_ref):
    piece = jnp.concatenate([piece_ref[slot_rows(i), :] for i in range(3)], axis=1)
    pair_hot = (join_col[...] == join_row[...]).astype(jnp.float32)
    slot_hot = (owner_col[...] == join_row[...]).astype(jnp.float32)
    pair_part = dot(pair_hot, piece, 1, 0)
    slot_part = dot(slot_hot, piece, 1, 0)
    norm = 0.0
    for i in range(3):
        cut = slice(i * HALF, (i + 1) * HALF)
        out_ref[slot_rows(i), :] = pair_part[:, cut]
        out_ref[slot_rows(3 + i), :] = slot_part[:, cut]
        weight = 2.0 if i == 1 else 1.0
        norm = norm + weight * slot_part[:, cut] * piece_ref[slot_rows(3 + i), :]
    norm = jnp.sum(jnp.sum(norm, axis=0, keepdims=True), axis=1, keepdims=True)
    out_ref[slot_rows(6), :] = jnp.broadcast_to(norm, (HALF, HALF))


def eliminate(work_ref, block):
    start = block * STEP
    shape = (STEP, HALF)
    rows = work_ref[start : start + STEP, :]
    left = [jnp.broadcast_to(rows[i : i + 1, :HALF], shape) for i in range(STEP)]
    right = [jnp.broadcast_to(rows[i : i + 1, HALF:], shape) for i in range(STEP)]
    lanes = [jnp.broadcast_to(rows[:, start + j : start + j + 1], shape) for j in range(STEP)]
    a = [[jnp.broadcast_to(lanes[j][i : i + 1, :], shape) for i in range(j + 1)] for j in range(STEP)]
    for k in range(STEP):
        root = lax.rsqrt(a[k][k])
        left[k] = left[k] * root
        right[k] = right[k] * root
        for j in range(k + 1, STEP):
            a[j][k] = a[j][k] * root
        for j in range(k + 1, STEP):
            for i in range(k + 1, j + 1):
                a[j][i] = a[j][i] - a[j][k] * a[i][k]
            left[j] = left[j] - a[j][k] * left[k]
            right[j] = right[j] - a[j][k] * right[k]
    sub = lax.broadcasted_iota(jnp.int32, shape, 0)
    lane = lax.broadcasted_iota(jnp.int32, shape, 1)
    one, two = left[0], right[0]
    for k in range(1, STEP):
        one = jnp.where(sub == k, left[k], one)
        two = jnp.where(sub == k, right[k], two)
    one = jnp.where(lane >= sub + start, one, 0.0)
    panel = jnp.concatenate([one, two], axis=1)
    work_ref[start : start + STEP, :] = panel
    if start + STEP < HALF:
        high = panel.astype(jnp.bfloat16).astype(jnp.float32)
        rest = panel - high
        middle = rest.astype(jnp.bfloat16).astype(jnp.float32)
        low = rest - middle
        lhs = jnp.concatenate([high, high, middle, middle, high, low], axis=0)[:, :HALF]
        rhs = jnp.concatenate([high, middle, high, middle, low, high], axis=0)
        update = lax.dot_general(
            lhs.astype(jnp.bfloat16),
            rhs.astype(jnp.bfloat16),
            (((0,), (0,)), ((), ())),
            preferred_element_type=jnp.float32,
        )
        work_ref[start + STEP :, :] = work_ref[start + STEP :, :] - update[start + STEP :, :]


def apply_kernel(
    entries, meta, column_lengths, join_row, rows_row, data_ref, gram_ref, out_ref, first, second, kept
):
    peers, depth, breadth = data_ref.shape
    here = depth - STEP
    live_pair = live_count(join_row, rows_row, column_lengths, meta[1])
    live_slot = live_count(join_row, rows_row, column_lengths, meta[2])
    sub = lax.broadcasted_iota(jnp.int32, (HALF, HALF), 0)
    lane = lax.broadcasted_iota(jnp.int32, (HALF, HALF), 1)
    eye = jnp.where(sub == lane, 1.0, 0.0)
    sub = sub.astype(jnp.float32)
    lane = lane.astype(jnp.float32)

    def masked(start, live, row_from, col_from):
        block = gram_ref[slot_rows(start), :]
        alive = jnp.logical_and(sub + row_from < live, lane + col_from < live)
        return jnp.where(alive, block, eye if row_from == col_from else 0.0)

    first[:, :HALF] = masked(0, live_pair, 0, 0)
    first[:, HALF:] = eye
    second[:, :HALF] = masked(3, live_slot, 0, 0)
    second[:, HALF:] = masked(4, live_slot, 0, HALF)

    def half(index, carry):
        for block in range(HALF // STEP):
            eliminate(first, block)
            eliminate(second, block)

        @pl.when(index == 0)
        def _():
            pair_turn = first[:, HALF:]
            pair_cross = dot(pair_turn, masked(1, live_pair, 0, HALF), 1, 0)
            slot_cross = second[:, HALF:]
            kept[:, :HALF] = pair_turn
            kept[:, HALF : 2 * HALF] = pair_cross
            kept[:, 2 * HALF : 4 * HALF] = second[...]
            first[:, :HALF] = masked(2, live_pair, HALF, HALF) - dot(
                pair_cross, pair_cross, 0, 0
            )
            first[:, HALF:] = eye
            second[:, :HALF] = masked(5, live_slot, HALF, HALF) - dot(
                slot_cross, slot_cross, 0, 0
            )

        return carry

    lax.fori_loop(0, 2, half, 0)

    column_ids = lax.broadcasted_iota(jnp.int32, (1, breadth), 1).astype(jnp.float32)
    site = data_ref[:, :here, :].reshape(peers * here, breadth)
    row_ids = lax.broadcasted_iota(jnp.int32, site.shape, 0)
    alive = jnp.logical_and(row_ids < meta[0], column_ids < live_pair)
    site = jnp.where(alive, site, 0.0)
    full_scale = math.sqrt(4 * peers * here)
    one = dot(site[:, :HALF], kept[:, :HALF], 1, 1)
    two = site[:, HALF:] - dot(one, kept[:, HALF : 2 * HALF], 1, 0)
    two = dot(two, first[:, HALF:], 1, 1)
    out_ref[:, :here, :HALF] = (full_scale * one).reshape(peers, here, HALF)
    out_ref[:, :here, HALF:] = (full_scale * two).reshape(peers, here, HALF)

    squares = jnp.sum(gram_ref[slot_rows(6), :], axis=0, keepdims=True)
    scale = lax.rsqrt(squares * (1.0 / entries) + 1e-06)
    nxt = data_ref[:, here:, :].reshape(peers * STEP, breadth)
    nxt = jnp.where(column_ids < live_slot, nxt, 0.0)
    one = dot(nxt[:, :HALF], kept[:, 2 * HALF : 3 * HALF], 1, 1) + dot(
        nxt[:, HALF:], kept[:, 3 * HALF :], 1, 1
    )
    two = dot(nxt[:, HALF:], second[:, :HALF], 1, 1)
    out_ref[:, here:, :HALF] = (scale * one).reshape(peers, STEP, HALF)
    out_ref[:, here:, HALF:] = (scale * two).reshape(peers, STEP, HALF)


def body(site_blocks, row_lengths, column_lengths, joining, owner_slots, next_blocks):
    sector_count, states, row_count, breadth = site_blocks.shape
    slots, local_columns = next_blocks.shape[:2]
    n_row = lax.axis_size("row")
    n_all = n_row * lax.axis_size("grp")
    both = ("grp", "row")
    me = lax.axis_index("grp") * n_row + lax.axis_index("row")
    quarters = n_row // slots
    piece_columns = local_columns // quarters
    sent = pl.pallas_call(
        gather_kernel,
        out_shape=jax.ShapeDtypeStruct((n_row, row_count + piece_columns, breadth), jnp.float32),
        in_specs=[HBM, HBM],
        out_specs=VMEM,
        scratch_shapes=[pltpu.SemaphoreType.DMA((2,))],
        compiler_params=PARAMS,
        name="gather",
    )(
        site_blocks.reshape(n_row, row_count, breadth),
        next_blocks.reshape(n_row, piece_columns, breadth),
    )
    join_flat = joining.reshape(-1)
    owner_flat = jnp.repeat(owner_slots, quarters)
    rows_flat = jnp.repeat(row_lengths, states)
    meta = jnp.stack([rows_flat[me], join_flat[me], owner_flat[me]])
    join_row = join_flat.reshape(1, n_all)
    join_col = join_flat.reshape(n_all, 1)
    owner_col = owner_flat.reshape(n_all, 1)
    rows_row = rows_flat.reshape(1, n_all).astype(jnp.float32)

    def swap(x):
        slots_of = x.reshape(n_all, SLOT, HALF)
        return lax.all_to_all(slots_of, both, 0, 0, tiled=True).reshape(x.shape)

    data = lax.all_to_all(sent, "row", 0, 0, tiled=True)
    gram = pl.pallas_call(
        gram_kernel,
        out_shape=jax.ShapeDtypeStruct((n_all * SLOT, HALF), jnp.float32),
        in_specs=[SMEM, SMEM, VMEM, VMEM, VMEM, VMEM, VMEM],
        out_specs=VMEM,
        compiler_params=PARAMS,
        name="gram",
    )(meta, column_lengths, join_row, rows_row, join_col, owner_col, data)
    pieces = swap(gram)
    rows = pl.pallas_call(
        combine_kernel,
        out_shape=jax.ShapeDtypeStruct((n_all * SLOT, HALF), jnp.float32),
        in_specs=[VMEM, VMEM, VMEM, VMEM],
        out_specs=VMEM,
        compiler_params=PARAMS,
        name="combine",
    )(join_row, join_col, owner_col, pieces)
    grams = swap(rows)
    entries = float(n_row * local_columns * breadth * slots * lax.axis_size("grp"))
    result = pl.pallas_call(
        functools.partial(apply_kernel, entries),
        out_shape=jax.ShapeDtypeStruct(sent.shape, jnp.float32),
        in_specs=[SMEM, SMEM, VMEM, VMEM, VMEM, VMEM],
        out_specs=VMEM,
        scratch_shapes=[
            pltpu.VMEM((HALF, 2 * HALF), jnp.float32),
            pltpu.VMEM((HALF, 2 * HALF), jnp.float32),
            pltpu.VMEM((HALF, 4 * HALF), jnp.float32),
        ],
        compiler_params=PARAMS,
        name="factor_apply",
    )(meta, column_lengths, join_row, rows_row, data, grams)
    back = lax.all_to_all(result, "row", 0, 0, tiled=True)
    canonical, next_site = pl.pallas_call(
        scatter_kernel,
        out_shape=(
            jax.ShapeDtypeStruct((n_row, row_count, breadth), jnp.float32),
            jax.ShapeDtypeStruct((n_row, piece_columns, breadth), jnp.float32),
        ),
        in_specs=[VMEM],
        out_specs=(HBM, HBM),
        scratch_shapes=[pltpu.SemaphoreType.DMA((2,))],
        compiler_params=PARAMS,
        name="scatter",
    )(back)
    canonical = canonical.reshape(site_blocks.shape)
    next_site = next_site.reshape(next_blocks.shape)
    return (canonical, next_site)


def solution(mesh):
    in_specs = (P("grp", None, "row", None), P(), P(), P(), P(), P("grp", "row", None))
    out_specs = (P("grp", None, "row", None), P("grp", "row", None))
    return jax.shard_map(body, mesh=mesh, in_specs=in_specs, out_specs=out_specs, check_vma=False)
```

time: 1470 us -> 102 us (0.07); the launches traced: 1440 us -> 101 us
  other arithmetic: 862 us -> 2.05 us
  matrix products: 269 us -> 0 us
  waiting for transfers between devices: 163 us -> 8.12 us
  local copies, waits for them, and re-layouts: 49.2 us -> 6.01 us
  Pallas kernels: 0 us -> 19.2 us
  loops' own time: 18.5 us -> 0 us
  between operations: 16 us -> 0.72 us
    reduce_sum x1027 -> x0, other arithmetic: 349 us -> none  [the longest x256 171 us: solve_step(): lower_row = jnp.sum(lower * select[None, :, None], axis=1)]
    sub x263 -> x0, other arithmetic: 349 us -> none  [the longest x256 341 us: cholesky_step(): work = work - current[:, :, None] * current[:, None, :]]
    dot_general x290 -> x0, matrix products: 269 us -> none  [the longest x256 171 us: solve_step(): combined = jnp.einsum('bj,bjk->bk', lower_row, inverse, precision=PRECISE)]
    psum x1 -> x0, waiting for transfers between devices: 163 us -> none  [body(): gram_total = lax.psum(gram_sheet, ('grp', 'row'))]
    add x258 -> x0, other arithmetic: 97.7 us -> none  [the longest x256 92.6 us: solve_step(): return inverse + select[None, :, None] * fresh[:, None, :]]
    psum x1 -> x0, blocking collectives: 64.5 us -> none  [body(): squares = lax.psum(jnp.sum(absorbed * absorbed), ('grp', 'row'))]
    all_to_all x0 -> x3, blocking collectives: none -> 55.8 us  [the longest x2 37.1 us: swap(): return lax.all_to_all(slots_of, both, 0, 0, tiled=True).reshape(x.shape)]
    transpose x2 -> x0, local copies, waits for them, and re-layouts: 20.6 us -> none  [factor(): return (jnp.swapaxes(lower, 1, 2), jnp.swapaxes(lower_inverse, 1, 2))]
  transfers between devices with their start and end apart: 1 -> 1, of which waited for: 1 -> 1; matrix products, arithmetic and copies ran while one was open for 0% -> 5% of each run, Pallas kernels for 0% -> 0%
where the time goes in v1:
time: 102 us; the launch traced here: 101 us
  blocking collectives  55.8 us (55%)
  Pallas kernels  19.2 us (19%)
  starting transfers between devices  9.43 us (9%)
  waiting for transfers between devices  8.12 us (8%)
  local copies, waits for them, and re-layouts  6.01 us (6%)
  other arithmetic  2.05 us (2%)
    all_to_all x2, blocking collectives, swap(): return lax.all_to_all(slots_of, both, 0, 0, tiled=True).reshape(x.shape)  37.1 us
    all_to_all x1, blocking collectives, body(): back = lax.all_to_all(result, 'row', 0, 0, tiled=True)  18.6 us
    pallas_call x1, Pallas kernels, body(): pl.pallas_call(functools.partial(apply_kernel, entries), out_shape=jax.Sh...  15.3 us
    all_to_all x1, starting transfers between devices, body(): data = lax.all_to_all(sent, 'row', 0, 0, tiled=True)  9.43 us
    all_to_all x1, waiting for transfers between devices, body(): data = lax.all_to_all(sent, 'row', 0, 0, tiled=True)  8.12 us
    unnamed x13, local copies, waits for them, and re-layouts  3.3 us
    another operation x1, other arithmetic, body(): meta = jnp.stack([rows_flat[me], join_flat[me], owner_flat[me]])  2.05 us
  transfers between devices with their start and end apart: 1, of which 1 were waited for; matrix products, arithmetic and copies ran while one was open for 5% of the time, Pallas kernels for 0%

profile of v1, /device:TPU:1, one launch (start us, length us, event | category | flops | bytes accessed | tf_op | source)
XLA Modules:
  0.0 101.3 jit_solution(11340821705993774874)
XLA Ops:
  0.6 1.0 %copy-done = f32[8,4,16,256]{3,2,1,0:T(8,128)S(1)} copy-done((f32[8,4,16,256]{3,2,1,0:T(8,128)S(1)}, f32[8,4,16,256]{3,2,1,0:T(8,128)}, u32[]{:S(2)}) %copy-start) | copy-done | bytes 524312
  1.7 0.9 copy-done.1
  2.6 1.0 gather.1
  3.6 0.0 copy-start.3
  3.6 9.4 %all-to-all-start = ((f32[32,24,256]{2,1,0:T(8,128)}), f32[32,24,256]{2,1,0:T(8,128)S(1)}, u32[]{:S(2)}, u32[]{:S(2)}) async-start(f32[32,24,256]{2,1,0:T(8,128)} %gather.1), calls=%async_computation | async-start | bytes 1572864 | tf_op jit(solution)/shard_map/all_to_all | solution.py:241
  13.1 0.1 copy.15
  13.1 0.1 reshape_reshape.10.join_row
  13.3 0.0 copy-start.4
  13.3 0.1 reshape.51
  13.4 0.5 copy-done.4
  13.9 0.1 broadcast_in_dim.9
  14.0 0.1 reshape.52
  14.1 0.1 reshape_reshape.14.unused_two.owner_col
  14.2 0.1 reshape_reshape.13.unused_one.join_col
  14.2 0.7 copy-done.5
  14.9 0.1 broadcast_in_dim.10
  15.0 0.1 convert_element_type.6.rows_row
  15.1 0.6 dynamic_slice.10
  15.7 0.6 dynamic_slice.11
  16.3 0.1 broadcast_in_dim.8
  16.3 0.1 reshape.50
  16.4 0.7 dynamic_slice.9
  17.1 2.0 %pad_add_fusion.meta = s32[3]{0:T(128)S(1)} fusion(s32[1]{0:T(128)} %dynamic_slice.11, s32[1]{0:T(128)} %dynamic_slice.10, s32[1]{0:T(128)} %dynamic_slice.9), kind=kLoop, calls=%fused_computation | loop fusion | flops 6 | bytes 24 | tf_op jit(solution)/shard_map/stack | solution.py:231
  19.2 8.1 %all-to-all-done.data_ref = f32[32,24,256]{2,1,0:T(8,128)S(1)} async-done(((f32[32,24,256]{2,1,0:T(8,128)}), f32[32,24,256]{2,1,0:T(8,128)S(1)}, u32[]{:S(2)}, u32[]{:S(2)}) %all-to-all-start) | async-done | bytes 786464 | tf_op jit(solution)/shard_map/all_to_all | solution.py:241
  27.3 0.0 copy-done.2
  27.3 1.4 %gram.1 = f32[1024,128]{1,0:T(8,128)S(1)} custom-call(s32[3]{0:T(128)S(1)} %pad_add_fusion.meta, s32[32]{0:T(128)S(1)} %copy-done.2, s32[1,128]{1,0:T(1,128)S(1)} %reshape_reshape.10.join_row, f32[1,128]{1,0:T(1,128)S(1)} %convert_element_type.6.rows_row, s32[128,1]{1,0:T(8,128)S(1)} %reshape_reshape.13.unused_one.join_col, ...), custom_call_target="tpu_custom_call" | custom-call | tf_op jit(solution)/shard_map/gram/pallas_call | solution.py:242
  28.7 19.2 %all_to_all.20 = f32[128,8,128]{2,1,0:T(8,128)S(1)} all-to-all(f32[128,8,128]{2,1,0:T(8,128)S(1)} %bitcast.11), channel_id=1, replica_groups=mesh['grp'=4,'row'=32] {'grp','row'}, dimensions={0} | all-to-all | bytes 1048576 | tf_op jit(solution)/shard_map/all_to_all | solution.py:239
  47.9 0.6 combine.1
  48.6 17.9 %all_to_all.21 = f32[128,8,128]{2,1,0:T(8,128)S(1)} all-to-all(f32[128,8,128]{2,1,0:T(8,128)S(1)} %bitcast.10), channel_id=1, replica_groups=mesh['grp'=4,'row'=32] {'grp','row'}, dimensions={0} | all-to-all | bytes 1048576 | tf_op jit(solution)/shard_map/all_to_all | solution.py:239
  66.5 15.3 %factor_apply.1 = f32[32,24,256]{2,1,0:T(8,128)S(1)} custom-call(s32[3]{0:T(128)S(1)} %pad_add_fusion.meta, s32[32]{0:T(128)S(1)} %copy-done.2, s32[1,128]{1,0:T(1,128)S(1)} %reshape_reshape.10.join_row, f32[1,128]{1,0:T(1,128)S(1)} %convert_element_type.6.rows_row, f32[32,24,256]{2,1,0:T(8,128)S(1)} %all-to-all-done.data_ref, f32[1024,128]{1,0:T(8,128)S(1)} %bitcast.8), custom_call_target="tpu_custom_call" | custom-call | tf_op jit(solution)/shard_map/factor_apply/pallas_call | solution.py:261
  81.8 18.6 %all_to_all.22.data_ref = f32[32,24,256]{2,1,0:T(8,128)S(1)} all-to-all(f32[32,24,256]{2,1,0:T(8,128)S(1)} %factor_apply.1), channel_id=1, replica_groups=mesh['grp'=4,'row'=32] {'row'}, dimensions={0} | all-to-all | bytes 1572864 | tf_op jit(solution)/shard_map/all_to_all | solution.py:274
  100.4 0.9 scatter.1
  (6 shorter events, 0.0 us)
Async XLA Ops:
  0.6 1.0 %copy-start = (f32[8,4,16,256]{3,2,1,0:T(8,128)S(1)}, f32[8,4,16,256]{3,2,1,0:T(8,128)}, u32[]{:S(2)}) copy-start(f32[8,4,16,256]{3,2,1,0:T(8,128)} %param.6) | copy-start | bytes 1572868
  1.7 0.9 copy-start.1
  3.6 9.5 %copy-start.3 = (s32[32,4]{0,1:T(4,128)S(1)}, s32[32,4]{0,1:T(4,128)}, u32[]{:S(2)}) copy-start(s32[32,4]{0,1:T(4,128)} %param.9) | copy-start | bytes 1540
  3.6 23.7 %all-to-all-start = ((f32[32,24,256]{2,1,0:T(8,128)}), f32[32,24,256]{2,1,0:T(8,128)S(1)}, u32[]{:S(2)}, u32[]{:S(2)}) async-start(f32[32,24,256]{2,1,0:T(8,128)} %gather.1), calls=%async_computation | async-start | bytes 1572864 | tf_op jit(solution)/shard_map/all_to_all | solution.py:241
  13.3 0.7 copy-start.4
  14.2 0.7 copy-start.5
  17.1 10.2 %copy-start.2 = (s32[32]{0:T(128)S(1)}, s32[32]{0:T(128)}, u32[]{:S(2)}) copy-start(s32[32]{0:T(128)} %column_lengths.3) | copy-start | bytes 388

commit v2 on v1

--- a/solution.py
+++ b/solution.py
@@ -11,7 +11,7 @@
 PRECISE = lax.Precision.HIGHEST
 HALF = 128
 STEP = 8
-SLOT = 8
+SLOT = 5
 HBM = pl.BlockSpec(memory_space=pltpu.HBM)
 PARAMS = pltpu.CompilerParams(vmem_limit_bytes=16 * 1024 * 1024)
 VMEM = pl.BlockSpec(memory_space=pltpu.VMEM)
@@ -64,72 +64,114 @@
     live_slot = live_count(join_row, rows_row, column_lengths, meta[2])
     column_ids = lax.broadcasted_iota(jnp.int32, (1, breadth), 1).astype(jnp.float32)
     nxt = jnp.where(column_ids < live_slot, nxt, 0.0)
-    for start, block in ((0, site), (3, nxt)):
+    sub = lax.broadcasted_iota(jnp.int32, (HALF, HALF), 0)
+    lane = lax.broadcasted_iota(jnp.int32, (HALF, HALF), 1)
+    diagonals = []
+    for start, block in ((0, site), (2, nxt)):
         top = dot(block[:, :HALF], block, 0, 0)
-        out_ref[slot_rows(start), :] = top[:, :HALF]
+        low = dot(block[:, HALF:], block[:, HALF:], 0, 0)
+        out_ref[slot_rows(start), :] = jnp.where(sub <= lane, top[:, :HALF], low)
         out_ref[slot_rows(start + 1), :] = top[:, HALF:]
-        out_ref[slot_rows(start + 2), :] = dot(block[:, HALF:], block[:, HALF:], 0, 0)
-
-
-def combine_kernel(join_row, join_col, owner_col, piece_ref, out_ref):
-    piece = jnp.concatenate([piece_ref[slot_rows(i), :] for i in range(3)], axis=1)
+        diagonals.append(jnp.sum(jnp.where(sub == lane, low, 0.0), axis=1, keepdims=True))
+    out_ref[slot_rows(4), :] = jnp.where(lane < HALF // 2, diagonals[0], diagonals[1])
+
+
+def combine_kernel(meta, join_row, join_col, owner_col, piece_ref, out_ref):
+    packed, cross, diagonal = (slice(i * HALF, (i + 1) * HALF) for i in range(3))
+    piece = jnp.concatenate([piece_ref[slot_rows(i), :] for i in (0, 1, 4)], axis=1)
     pair_hot = (join_col[...] == join_row[...]).astype(jnp.float32)
     slot_hot = (owner_col[...] == join_row[...]).astype(jnp.float32)
     pair_part = dot(pair_hot, piece, 1, 0)
     slot_part = dot(slot_hot, piece, 1, 0)
-    norm = 0.0
-    for i in range(3):
-        cut = slice(i * HALF, (i + 1) * HALF)
-        out_ref[slot_rows(i), :] = pair_part[:, cut]
-        out_ref[slot_rows(3 + i), :] = slot_part[:, cut]
-        weight = 2.0 if i == 1 else 1.0
-        norm = norm + weight * slot_part[:, cut] * piece_ref[slot_rows(3 + i), :]
+    out_ref[slot_rows(0), :] = pair_part[:, packed]
+    out_ref[slot_rows(1), :] = pair_part[:, cross]
+    out_ref[slot_rows(2), :] = slot_part[:, packed]
+    out_ref[slot_rows(3), :] = slot_part[:, cross]
+    lane = lax.broadcasted_iota(jnp.int32, (1, HALF), 1)
+    norm = jnp.where(lane == meta[3], 1.0, 2.0) * slot_part[:, packed] * piece_ref[slot_rows(2), :]
+    norm = norm + 2.0 * slot_part[:, cross] * piece_ref[slot_rows(3), :]
+    moment = jnp.where(lane == HALF - 1, pltpu.roll(slot_part[:, diagonal], HALF // 2, 1), 0.0)
+    norm = norm + moment * piece_ref[slot_rows(4), :]
     norm = jnp.sum(jnp.sum(norm, axis=0, keepdims=True), axis=1, keepdims=True)
-    out_ref[slot_rows(6), :] = jnp.broadcast_to(norm, (HALF, HALF))
-
-
-def eliminate(work_ref, block):
-    start = block * STEP
+    quarter = HALF // 4
+    pair_diagonal = jnp.broadcast_to(pair_part[:, 2 * HALF : 2 * HALF + 1], (HALF, HALF))
+    slot_diagonal = jnp.broadcast_to(slot_part[:, 2 * HALF : 2 * HALF + 1], (HALF, HALF))
+    last = jnp.where(lane < quarter, pair_diagonal, slot_diagonal)
+    out_ref[slot_rows(4), :] = jnp.where(lane < 2 * quarter, last, norm)
+
+
+def split(x):
+    high = x.astype(jnp.bfloat16).astype(jnp.float32)
+    rest = x - high
+    middle = rest.astype(jnp.bfloat16).astype(jnp.float32)
+    return high, middle, rest - middle
+
+
+def eliminate(first, second):
     shape = (STEP, HALF)
-    rows = work_ref[start : start + STEP, :]
-    left = [jnp.broadcast_to(rows[i : i + 1, :HALF], shape) for i in range(STEP)]
-    right = [jnp.broadcast_to(rows[i : i + 1, HALF:], shape) for i in range(STEP)]
-    lanes = [jnp.broadcast_to(rows[:, start + j : start + j + 1], shape) for j in range(STEP)]
-    a = [[jnp.broadcast_to(lanes[j][i : i + 1, :], shape) for i in range(j + 1)] for j in range(STEP)]
-    for k in range(STEP):
-        root = lax.rsqrt(a[k][k])
-        left[k] = left[k] * root
-        right[k] = right[k] * root
-        for j in range(k + 1, STEP):
-            a[j][k] = a[j][k] * root
-        for j in range(k + 1, STEP):
-            for i in range(k + 1, j + 1):
-                a[j][i] = a[j][i] - a[j][k] * a[i][k]
-            left[j] = left[j] - a[j][k] * left[k]
-            right[j] = right[j] - a[j][k] * right[k]
     sub = lax.broadcasted_iota(jnp.int32, shape, 0)
     lane = lax.broadcasted_iota(jnp.int32, shape, 1)
-    one, two = left[0], right[0]
-    for k in range(1, STEP):
-        one = jnp.where(sub == k, left[k], one)
-        two = jnp.where(sub == k, right[k], two)
-    one = jnp.where(lane >= sub + start, one, 0.0)
-    panel = jnp.concatenate([one, two], axis=1)
-    work_ref[start : start + STEP, :] = panel
-    if start + STEP < HALF:
-        high = panel.astype(jnp.bfloat16).astype(jnp.float32)
-        rest = panel - high
-        middle = rest.astype(jnp.bfloat16).astype(jnp.float32)
-        low = rest - middle
-        lhs = jnp.concatenate([high, high, middle, middle, high, low], axis=0)[:, :HALF]
-        rhs = jnp.concatenate([high, middle, high, middle, low, high], axis=0)
-        update = lax.dot_general(
-            lhs.astype(jnp.bfloat16),
-            rhs.astype(jnp.bfloat16),
-            (((0,), (0,)), ((), ())),
-            preferred_element_type=jnp.float32,
-        )
-        work_ref[start + STEP :, :] = work_ref[start + STEP :, :] - update[start + STEP :, :]
+    upper_half = sub < STEP // 2
+
+    def load(row, side):
+        cut = slice(side * HALF, (side + 1) * HALF)
+        one = jnp.broadcast_to(first[row : row + 1, cut], shape)
+        two = jnp.broadcast_to(second[row : row + 1, cut], shape)
+        return jnp.where(upper_half, one, two)
+
+    def spread(x, column):
+        return jnp.broadcast_to(x[:, column : column + 1], shape)
+
+    sides = [[load(i, side) for i in range(STEP)] for side in (0, 1)]
+    for start in range(0, HALF, STEP):
+        after = start + STEP
+        a = [[spread(sides[0][i], start + j) for i in range(j + 1)] for j in range(STEP)]
+        following = None
+        if after < HALF:
+            following = [[load(after + i, side) for i in range(STEP)] for side in (0, 1)]
+        for k in range(STEP):
+            root = lax.rsqrt(a[k][k])
+            for j in range(k + 1, STEP):
+                a[j][k] = a[j][k] * root
+            for j in range(k + 1, STEP):
+                for i in range(k + 1, j + 1):
+                    a[j][i] = a[j][i] - a[j][k] * a[i][k]
+            for rows in sides:
+                rows[k] = rows[k] * root
+                for j in range(k + 1, STEP):
+                    rows[j] = rows[j] - a[j][k] * rows[k]
+            if following is not None:
+                for i in range(STEP):
+                    factor = spread(sides[0][k], after + i)
+                    for rows, later in zip(sides, following):
+                        later[i] = later[i] - factor * rows[k]
+
+        panels = [[], []]
+        for rows in sides:
+            straight, crossed = rows[0], rows[STEP // 2]
+            for k in range(1, STEP):
+                straight = jnp.where(sub == k, rows[k], straight)
+                crossed = jnp.where(sub == k, rows[(k + STEP // 2) % STEP], crossed)
+            crossed = pltpu.roll(crossed, STEP // 2, 0)
+            panels[0].append(jnp.where(upper_half, straight, crossed))
+            panels[1].append(jnp.where(upper_half, crossed, straight))
+        for work_ref, (one, two) in zip((first, second), panels):
+            one = jnp.where(lane >= sub + start, one, 0.0)
+            panel = jnp.concatenate([one, two], axis=1)
+            work_ref[start:after, :] = panel
+            if after + STEP < HALF:
+                high, middle, low = split(panel)
+                lhs = jnp.concatenate([high, high, middle, middle, high, low], axis=0)[:, :HALF]
+                rhs = jnp.concatenate([high, middle, high, middle, low, high], axis=0)
+                update = lax.dot_general(
+                    lhs.astype(jnp.bfloat16),
+                    rhs.astype(jnp.bfloat16),
+                    (((0,), (0,)), ((), ())),
+                    preferred_element_type=jnp.float32,
+                )
+                rest = slice(after + STEP, HALF)
+                work_ref[rest, :] = work_ref[rest, :] - update[rest, :]
+        sides = following
 
 
 def apply_kernel(
@@ -145,20 +187,23 @@
     sub = sub.astype(jnp.float32)
     lane = lane.astype(jnp.float32)
 
+    lasts = gram_ref[slot_rows(4), :]
+
     def masked(start, live, row_from, col_from):
         block = gram_ref[slot_rows(start), :]
+        if row_from:
+            column = start * HALF // 8
+            block = jnp.where(sub == lane, lasts[:, column : column + 1], block.T)
         alive = jnp.logical_and(sub + row_from < live, lane + col_from < live)
         return jnp.where(alive, block, eye if row_from == col_from else 0.0)
 
     first[:, :HALF] = masked(0, live_pair, 0, 0)
     first[:, HALF:] = eye
-    second[:, :HALF] = masked(3, live_slot, 0, 0)
-    second[:, HALF:] = masked(4, live_slot, 0, HALF)
+    second[:, :HALF] = masked(2, live_slot, 0, 0)
+    second[:, HALF:] = masked(3, live_slot, 0, HALF)
 
     def half(index, carry):
-        for block in range(HALF // STEP):
-            eliminate(first, block)
-            eliminate(second, block)
+        eliminate(first, second)
 
         @pl.when(index == 0)
         def _():
@@ -168,11 +213,11 @@
             kept[:, :HALF] = pair_turn
             kept[:, HALF : 2 * HALF] = pair_cross
             kept[:, 2 * HALF : 4 * HALF] = second[...]
-            first[:, :HALF] = masked(2, live_pair, HALF, HALF) - dot(
+            first[:, :HALF] = masked(0, live_pair, HALF, HALF) - dot(
                 pair_cross, pair_cross, 0, 0
             )
             first[:, HALF:] = eye
-            second[:, :HALF] = masked(5, live_slot, HALF, HALF) - dot(
+            second[:, :HALF] = masked(2, live_slot, HALF, HALF) - dot(
                 slot_cross, slot_cross, 0, 0
             )
 
@@ -192,7 +237,7 @@
     out_ref[:, :here, :HALF] = (full_scale * one).reshape(peers, here, HALF)
     out_ref[:, :here, HALF:] = (full_scale * two).reshape(peers, here, HALF)
 
-    squares = jnp.sum(gram_ref[slot_rows(6), :], axis=0, keepdims=True)
+    squares = jnp.sum(lasts, axis=0, keepdims=True)[:, HALF - 1 :]
     scale = lax.rsqrt(squares * (1.0 / entries) + 1e-06)
     nxt = data_ref[:, here:, :].reshape(peers * STEP, breadth)
     nxt = jnp.where(column_ids < live_slot, nxt, 0.0)
@@ -228,14 +273,14 @@
     join_flat = joining.reshape(-1)
     owner_flat = jnp.repeat(owner_slots, quarters)
     rows_flat = jnp.repeat(row_lengths, states)
-    meta = jnp.stack([rows_flat[me], join_flat[me], owner_flat[me]])
+    meta = jnp.stack([rows_flat[me], join_flat[me], owner_flat[me], me])
     join_row = join_flat.reshape(1, n_all)
     join_col = join_flat.reshape(n_all, 1)
     owner_col = owner_flat.reshape(n_all, 1)
     rows_row = rows_flat.reshape(1, n_all).astype(jnp.float32)
 
     def swap(x):
-        slots_of = x.reshape(n_all, SLOT, HALF)
+        slots_of = x.reshape(n_all, 1, SLOT * HALF)
         return lax.all_to_all(slots_of, both, 0, 0, tiled=True).reshape(x.shape)
 
     data = lax.all_to_all(sent, "row", 0, 0, tiled=True)
@@ -251,11 +296,11 @@
     rows = pl.pallas_call(
         combine_kernel,
         out_shape=jax.ShapeDtypeStruct((n_all * SLOT, HALF), jnp.float32),
-        in_specs=[VMEM, VMEM, VMEM, VMEM],
+        in_specs=[SMEM, VMEM, VMEM, VMEM, VMEM],
         out_specs=VMEM,
         compiler_params=PARAMS,
         name="combine",
-    )(join_row, join_col, owner_col, pieces)
+    )(meta, join_row, join_col, owner_col, pieces)
     grams = swap(rows)
     entries = float(n_row * local_columns * breadth * slots * lax.axis_size("grp"))
     result = pl.pallas_call(

time: 102 us -> 94.1 us (0.923)
  blocking collectives: 55.8 us -> 51.7 us
  Pallas kernels: 19.2 us -> 15.7 us
    pallas_call x1, Pallas kernels: 15.3 us -> 11.1 us  [body(): pl.pallas_call(functools.partial(apply_kernel, entries), out_shape=jax.Sh...]
    all_to_all x2, blocking collectives: 37.1 us -> 33 us  [swap(): return lax.all_to_all(slots_of, both, 0, 0, tiled=True).reshape(x.shape)]
where the time goes in v2:
time: 94.1 us; the launch traced here: 93.7 us
  blocking collectives  51.7 us (55%)
  Pallas kernels  15.7 us (17%)
  starting transfers between devices  9.43 us (10%)
  waiting for transfers between devices  8.09 us (9%)
  local copies, waits for them, and re-layouts  6.07 us (6%)
  other arithmetic  2.03 us (2%)
    all_to_all x2, blocking collectives, swap(): return lax.all_to_all(slots_of, both, 0, 0, tiled=True).reshape(x.shape)  33 us
    all_to_all x1, blocking collectives, body(): back = lax.all_to_all(result, 'row', 0, 0, tiled=True)  18.6 us
    pallas_call x1, Pallas kernels, body(): pl.pallas_call(functools.partial(apply_kernel, entries), out_shape=jax.Sh...  11.1 us
    all_to_all x1, starting transfers between devices, body(): data = lax.all_to_all(sent, 'row', 0, 0, tiled=True)  9.43 us
    all_to_all x1, waiting for transfers between devices, body(): data = lax.all_to_all(sent, 'row', 0, 0, tiled=True)  8.09 us
    unnamed x13, local copies, waits for them, and re-layouts  3.3 us
    another operation x1, other arithmetic, body(): meta = jnp.stack([rows_flat[me], join_flat[me], owner_flat[me], me])  2.02 us
    dynamic_slice x3, local copies, waits for them, and re-layouts, body(): meta = jnp.stack([rows_flat[me], join_flat[me], owner_flat[me], me])  1.89 us
  transfers between devices with their start and end apart: 1, of which 1 were waited for; matrix products, arithmetic and copies ran while one was open for 5% of the time, Pallas kernels for 0%

profile of v2, /device:TPU:1, one launch (start us, length us, event | category | flops | bytes accessed | tf_op | source)
XLA Modules:
  0.0 93.7 jit_solution(1410039557686890311)
XLA Ops:
  0.6 1.0 %copy-done = f32[8,4,16,256]{3,2,1,0:T(8,128)S(1)} copy-done((f32[8,4,16,256]{3,2,1,0:T(8,128)S(1)}, f32[8,4,16,256]{3,2,1,0:T(8,128)}, u32[]{:S(2)}) %copy-start) | copy-done | bytes 524312
  1.7 0.9 %copy-done.1 = f32[8,32,256]{2,1,0:T(8,128)S(1)} copy-done((f32[8,32,256]{2,1,0:T(8,128)S(1)}, f32[8,32,256]{2,1,0:T(8,128)}, u32[]{:S(2)}) %copy-start.1) | copy-done | bytes 262168
  2.6 1.0 %gather.1 = f32[32,24,256]{2,1,0:T(8,128)} custom-call(f32[32,16,256]{2,1,0:T(8,128)S(1)} %bitcast.13, f32[32,8,256]{2,1,0:T(8,128)S(1)} %bitcast.14), custom_call_target="tpu_custom_call" | custom-call | tf_op jit(solution)/shard_map/gather/pallas_call | solution.py:261
  3.6 0.0 copy-start.3
  3.6 9.4 %all-to-all-start = ((f32[32,24,256]{2,1,0:T(8,128)}), f32[32,24,256]{2,1,0:T(8,128)S(1)}, u32[]{:S(2)}, u32[]{:S(2)}) async-start(f32[32,24,256]{2,1,0:T(8,128)} %gather.1), calls=%async_computation | async-start | bytes 1572864 | tf_op jit(solution)/shard_map/all_to_all | solution.py:286
  13.0 0.0 copy-done.3
  13.1 0.1 copy.22
  13.1 0.1 reshape_reshape.10.join_row
  13.3 0.0 copy-start.4
  13.3 0.1 reshape.51
  13.4 0.5 copy-done.4
  13.9 0.1 broadcast_in_dim.9
  14.0 0.1 reshape.52
  14.1 0.1 reshape_reshape.14.unused_two.owner_col
  14.2 0.1 reshape_reshape.13.unused_one.join_col
  14.2 0.7 copy-done.5
  14.9 0.1 broadcast_in_dim.10
  15.0 0.1 convert_element_type.6.rows_row
  15.1 0.7 dynamic_slice.10
  15.7 0.6 dynamic_slice.11
  16.3 0.1 broadcast_in_dim.8
  16.4 0.1 reshape.50
  16.5 0.7 dynamic_slice.9
  17.2 2.0 %pad_add_fusion.meta = s32[4]{0:T(128)S(1)} fusion(s32[1]{0:T(128)} %bitcast, s32[1]{0:T(128)} %dynamic_slice.11, s32[1]{0:T(128)} %dynamic_slice.10, s32[1]{0:T(128)} %dynamic_slice.9), kind=kLoop, calls=%fused_computation | loop fusion | flops 12 | bytes 32 | tf_op jit(solution)/shard_map/stack | solution.py:276
  19.2 8.1 %all-to-all-done.data_ref = f32[32,24,256]{2,1,0:T(8,128)S(1)} async-done(((f32[32,24,256]{2,1,0:T(8,128)}), f32[32,24,256]{2,1,0:T(8,128)S(1)}, u32[]{:S(2)}, u32[]{:S(2)}) %all-to-all-start) | async-done | bytes 786464 | tf_op jit(solution)/shard_map/all_to_all | solution.py:286
  27.3 1.5 %gram.1 = f32[640,128]{1,0:T(8,128)S(1)} custom-call(s32[4]{0:T(128)S(1)} %pad_add_fusion.meta, s32[32]{0:T(128)S(1)} %copy-done.2, s32[1,128]{1,0:T(1,128)S(1)} %reshape_reshape.10.join_row, f32[1,128]{1,0:T(1,128)S(1)} %convert_element_type.6.rows_row, s32[128,1]{1,0:T(8,128)S(1)} %reshape_reshape.13.unused_one.join_col, ...), custom_call_target="tpu_custom_call" | custom-call | tf_op jit(solution)/shard_map/gram/pallas_call | solution.py:287
  28.8 17.2 %all_to_all.20 = f32[128,1,640]{2,1,0:T(1,128)S(1)} all-to-all(f32[128,1,640]{2,1,0:T(1,128)S(1)} %bitcast.12), channel_id=1, replica_groups=mesh['grp'=4,'row'=32] {'grp','row'}, dimensions={0} | all-to-all | bytes 655360 | tf_op jit(solution)/shard_map/all_to_all | solution.py:284
  46.0 1.2 %combine.1 = f32[640,128]{1,0:T(8,128)S(1)} custom-call(s32[4]{0:T(128)S(1)} %pad_add_fusion.meta, s32[1,128]{1,0:T(1,128)S(1)} %reshape_reshape.10.join_row, s32[128,1]{1,0:T(8,128)S(1)} %reshape_reshape.13.unused_one.join_col, s32[128,1]{1,0:T(8,128)S(1)} %reshape_reshape.14.unused_two.owner_col, f32[640,128]{1,0:T(8,128)S(1)} %bitcast.9), custom_call_target="tpu_custom_call" | custom-call | tf_op jit(solution)/shard_map/combine/pallas_call | solution.py:296
  47.2 15.9 %all_to_all.21 = f32[128,1,640]{2,1,0:T(1,128)S(1)} all-to-all(f32[128,1,640]{2,1,0:T(1,128)S(1)} %bitcast.10), channel_id=1, replica_groups=mesh['grp'=4,'row'=32] {'grp','row'}, dimensions={0} | all-to-all | bytes 655360 | tf_op jit(solution)/shard_map/all_to_all | solution.py:284
  63.1 11.1 %factor_apply.1 = f32[32,24,256]{2,1,0:T(8,128)S(1)} custom-call(s32[4]{0:T(128)S(1)} %pad_add_fusion.meta, s32[32]{0:T(128)S(1)} %copy-done.2, s32[1,128]{1,0:T(1,128)S(1)} %reshape_reshape.10.join_row, f32[1,128]{1,0:T(1,128)S(1)} %convert_element_type.6.rows_row, f32[32,24,256]{2,1,0:T(8,128)S(1)} %all-to-all-done.data_ref, f32[640,128]{1,0:T(8,128)S(1)} %bitcast.11), custom_call_target="tpu_custom_call" | custom-call | tf_op jit(solution)/shard_map/factor_apply/pallas_call | solution.py:306
  74.2 18.6 %all_to_all.22.data_ref = f32[32,24,256]{2,1,0:T(8,128)S(1)} all-to-all(f32[32,24,256]{2,1,0:T(8,128)S(1)} %factor_apply.1), channel_id=1, replica_groups=mesh['grp'=4,'row'=32] {'row'}, dimensions={0} | all-to-all | bytes 1572864 | tf_op jit(solution)/shard_map/all_to_all | solution.py:319
  92.8 0.9 scatter.1
  (6 shorter events, 0.0 us)
Async XLA Ops:
  0.6 1.0 %copy-start = (f32[8,4,16,256]{3,2,1,0:T(8,128)S(1)}, f32[8,4,16,256]{3,2,1,0:T(8,128)}, u32[]{:S(2)}) copy-start(f32[8,4,16,256]{3,2,1,0:T(8,128)} %param.6) | copy-start | bytes 1572868
  1.7 0.9 %copy-start.1 = (f32[8,32,256]{2,1,0:T(8,128)S(1)}, f32[8,32,256]{2,1,0:T(8,128)}, u32[]{:S(2)}) copy-start(f32[8,32,256]{2,1,0:T(8,128)} %param.11) | copy-start | bytes 786436
  3.6 9.5 %copy-start.3 = (s32[32,4]{0,1:T(4,128)S(1)}, s32[32,4]{0,1:T(4,128)}, u32[]{:S(2)}) copy-start(s32[32,4]{0,1:T(4,128)} %param.9) | copy-start | bytes 1540
  3.6 23.7 %all-to-all-start = ((f32[32,24,256]{2,1,0:T(8,128)}), f32[32,24,256]{2,1,0:T(8,128)S(1)}, u32[]{:S(2)}, u32[]{:S(2)}) async-start(f32[32,24,256]{2,1,0:T(8,128)} %gather.1), calls=%async_computation | async-start | bytes 1572864 | tf_op jit(solution)/shard_map/all_to_all | solution.py:286
  13.3 0.7 copy-start.4
  14.2 0.7 copy-start.5
  17.2 10.1 %copy-start.2 = (s32[32]{0:T(128)S(1)}, s32[32]{0:T(128)}, u32[]{:S(2)}) copy-start(s32[32]{0:T(128)} %column_lengths.3) | copy-start | bytes 388

commit v3 on v2

--- a/solution.py
+++ b/solution.py
@@ -12,6 +12,8 @@
 HALF = 128
 STEP = 8
 SLOT = 5
+WHEN = 4
+SHARES = 4
 HBM = pl.BlockSpec(memory_space=pltpu.HBM)
 PARAMS = pltpu.CompilerParams(vmem_limit_bytes=16 * 1024 * 1024)
 VMEM = pl.BlockSpec(memory_space=pltpu.VMEM)
@@ -30,14 +32,27 @@
     return jnp.minimum(jnp.floor(joined * 0.5), column_lengths[sector].astype(jnp.float32))
 
 
-def gather_kernel(site_ref, next_ref, out_ref, sems):
+def gather_kernel(site_ref, next_ref, out_ref, held, in_sems, out_sems):
     here = site_ref.shape[1]
-    one = pltpu.make_async_copy(site_ref, out_ref.at[:, :here, :], sems.at[0])
-    two = pltpu.make_async_copy(next_ref, out_ref.at[:, here:, :], sems.at[1])
-    one.start()
-    two.start()
-    one.wait()
-    two.wait()
+    share = site_ref.shape[0] // SHARES
+    cuts = [pl.ds(i * share, share) for i in range(SHARES)]
+    arrivals = [
+        (
+            pltpu.make_async_copy(site_ref.at[cut], held.at[cut, :here, :], in_sems.at[i, 0]),
+            pltpu.make_async_copy(next_ref.at[cut], held.at[cut, here:, :], in_sems.at[i, 1]),
+        )
+        for i, cut in enumerate(cuts)
+    ]
+    leaves = [pltpu.make_async_copy(held.at[cut], out_ref.at[cut], out_sems.at[i]) for i, cut in enumerate(cuts)]
+    for pair in arrivals:
+        pair[0].start()
+        pair[1].start()
+    for pair, leave in zip(arrivals, leaves):
+        pair[0].wait()
+        pair[1].wait()
+        leave.start()
+    for leave in leaves:
+        leave.wait()
 
 
 def scatter_kernel(data_ref, site_ref, next_ref, sems):
@@ -76,13 +91,27 @@
     out_ref[slot_rows(4), :] = jnp.where(lane < HALF // 2, diagonals[0], diagonals[1])
 
 
+def split(x):
+    high = x.astype(jnp.bfloat16).astype(jnp.float32)
+    rest = x - high
+    middle = rest.astype(jnp.bfloat16).astype(jnp.float32)
+    return high, middle, rest - middle
+
+
 def combine_kernel(meta, join_row, join_col, owner_col, piece_ref, out_ref):
     packed, cross, diagonal = (slice(i * HALF, (i + 1) * HALF) for i in range(3))
     piece = jnp.concatenate([piece_ref[slot_rows(i), :] for i in (0, 1, 4)], axis=1)
-    pair_hot = (join_col[...] == join_row[...]).astype(jnp.float32)
-    slot_hot = (owner_col[...] == join_row[...]).astype(jnp.float32)
-    pair_part = dot(pair_hot, piece, 1, 0)
-    slot_part = dot(slot_hot, piece, 1, 0)
+    hot = jnp.concatenate([join_col[...] == join_row[...], owner_col[...] == join_row[...]], axis=0)
+    hot = hot.astype(jnp.float32).astype(jnp.bfloat16)
+    parts = 0.0
+    for part in split(piece)[::-1]:
+        parts = parts + lax.dot_general(
+            hot,
+            part.astype(jnp.bfloat16),
+            (((1,), (0,)), ((), ())),
+            preferred_element_type=jnp.float32,
+        )
+    pair_part, slot_part = parts[:HALF], parts[HALF:]
     out_ref[slot_rows(0), :] = pair_part[:, packed]
     out_ref[slot_rows(1), :] = pair_part[:, cross]
     out_ref[slot_rows(2), :] = slot_part[:, packed]
@@ -100,14 +129,24 @@
     out_ref[slot_rows(4), :] = jnp.where(lane < 2 * quarter, last, norm)
 
 
-def split(x):
-    high = x.astype(jnp.bfloat16).astype(jnp.float32)
-    rest = x - high
-    middle = rest.astype(jnp.bfloat16).astype(jnp.float32)
-    return high, middle, rest - middle
-
-
-def eliminate(first, second):
+def product(x, w, contract):
+    parts = [p.astype(jnp.bfloat16) for p in split(x)]
+    high, middle, low = (p.astype(jnp.bfloat16) for p in split(w))
+    wide = jnp.concatenate([parts[0], parts[1]], axis=1)
+    tall = jnp.concatenate([parts[0], parts[2]], axis=1)
+    inner, outer = contract, 1 - contract
+    one = jnp.concatenate(
+        [jnp.concatenate([p, p], axis=inner) for p in (high, middle)], axis=outer
+    )
+    two = jnp.concatenate([low, high], axis=inner)
+    dims = (((1,), (inner,)), ((), ()))
+    main = lax.dot_general(wide, one, dims, preferred_element_type=jnp.float32)
+    rest = lax.dot_general(tall, two, dims, preferred_element_type=jnp.float32)
+    width = w.shape[outer]
+    return main[:, :width] + (main[:, width:] + rest)
+
+
+def eliminate(first, second, turn):
     shape = (STEP, HALF)
     sub = lax.broadcasted_iota(jnp.int32, shape, 0)
     lane = lax.broadcasted_iota(jnp.int32, shape, 1)
@@ -122,30 +161,8 @@
     def spread(x, column):
         return jnp.broadcast_to(x[:, column : column + 1], shape)
 
-    sides = [[load(i, side) for i in range(STEP)] for side in (0, 1)]
-    for start in range(0, HALF, STEP):
+    def finish(start, sides):
         after = start + STEP
-        a = [[spread(sides[0][i], start + j) for i in range(j + 1)] for j in range(STEP)]
-        following = None
-        if after < HALF:
-            following = [[load(after + i, side) for i in range(STEP)] for side in (0, 1)]
-        for k in range(STEP):
-            root = lax.rsqrt(a[k][k])
-            for j in range(k + 1, STEP):
-                a[j][k] = a[j][k] * root
-            for j in range(k + 1, STEP):
-                for i in range(k + 1, j + 1):
-                    a[j][i] = a[j][i] - a[j][k] * a[i][k]
-            for rows in sides:
-                rows[k] = rows[k] * root
-                for j in range(k + 1, STEP):
-                    rows[j] = rows[j] - a[j][k] * rows[k]
-            if following is not None:
-                for i in range(STEP):
-                    factor = spread(sides[0][k], after + i)
-                    for rows, later in zip(sides, following):
-                        later[i] = later[i] - factor * rows[k]
-
         panels = [[], []]
         for rows in sides:
             straight, crossed = rows[0], rows[STEP // 2]
@@ -163,19 +180,69 @@
                 high, middle, low = split(panel)
                 lhs = jnp.concatenate([high, high, middle, middle, high, low], axis=0)[:, :HALF]
                 rhs = jnp.concatenate([high, middle, high, middle, low, high], axis=0)
+                base = (after + STEP) // 16 * 16
                 update = lax.dot_general(
-                    lhs.astype(jnp.bfloat16),
+                    lhs.astype(jnp.bfloat16).T[base:],
                     rhs.astype(jnp.bfloat16),
-                    (((0,), (0,)), ((), ())),
+                    (((1,), (0,)), ((), ())),
                     preferred_element_type=jnp.float32,
                 )
                 rest = slice(after + STEP, HALF)
-                work_ref[rest, :] = work_ref[rest, :] - update[rest, :]
-        sides = following
+                work_ref[rest, :] = work_ref[rest, :] - update[after + STEP - base :, :]
+
+    quad = STEP // 2
+    sides = [[load(i, side) for i in range(STEP)] for side in (0, 1)]
+    done = None
+    for start in range(0, HALF, STEP):
+        after = start + STEP
+        a = [[spread(sides[0][i], start + j) for i in range(j + 1)] for j in range(STEP)]
+        following = None
+        for k in range(STEP):
+            root = lax.rsqrt(a[k][k])
+            for j in range(k + 1, STEP):
+                a[j][k] = a[j][k] * root
+            for j in range(k + 1, STEP):
+                for i in range(k + 1, j + 1):
+                    a[j][i] = a[j][i] - a[j][k] * a[i][k]
+            for rows in sides:
+                rows[k] = rows[k] * root
+                for j in range(k + 1, STEP):
+                    rows[j] = rows[j] - a[j][k] * rows[k]
+            if k == WHEN and done is not None:
+                finish(*done)
+            if after < HALF:
+                if following is None:
+                    totals = [[None, None], [None, None]]
+                    following = True
+                for part in (0, 1):
+                    index = after + part * quad + sub % quad
+                    factor = jnp.take_along_axis(sides[0][k], index, axis=1)
+                    for rows, total in zip(sides, totals):
+                        term = factor * rows[k]
+                        total[part] = term if k == 0 else total[part] + term
+        done = (start, sides)
+        if after < HALF:
+            for side in (0, 1):
+                cut = slice(side * HALF, (side + 1) * HALF)
+                one, two = first[after : after + STEP, cut], second[after : after + STEP, cut]
+                early = jnp.where(upper_half, one, pltpu.roll(two, quad, 0))
+                late = jnp.where(upper_half, pltpu.roll(one, quad, 0), two)
+                turn[:STEP, cut] = early - totals[side][0]
+                turn[STEP:, cut] = late - totals[side][1]
+
+            def reload(i, side):
+                cut = slice(side * HALF, (side + 1) * HALF)
+                row = i // quad * STEP + i % quad
+                one = jnp.broadcast_to(turn[row : row + 1, cut], shape)
+                two = jnp.broadcast_to(turn[row + quad : row + quad + 1, cut], shape)
+                return jnp.where(upper_half, one, two)
+
+            sides = [[reload(i, side) for i in range(STEP)] for side in (0, 1)]
+    finish(*done)
 
 
 def apply_kernel(
-    entries, meta, column_lengths, join_row, rows_row, data_ref, gram_ref, out_ref, first, second, kept
+    entries, meta, column_lengths, join_row, rows_row, data_ref, gram_ref, out_ref, first, second, kept, turn
 ):
     peers, depth, breadth = data_ref.shape
     here = depth - STEP
@@ -203,7 +270,7 @@
     second[:, HALF:] = masked(3, live_slot, 0, HALF)
 
     def half(index, carry):
-        eliminate(first, second)
+        eliminate(first, second, turn)
 
         @pl.when(index == 0)
         def _():
@@ -231,9 +298,9 @@
     alive = jnp.logical_and(row_ids < meta[0], column_ids < live_pair)
     site = jnp.where(alive, site, 0.0)
     full_scale = math.sqrt(4 * peers * here)
-    one = dot(site[:, :HALF], kept[:, :HALF], 1, 1)
-    two = site[:, HALF:] - dot(one, kept[:, HALF : 2 * HALF], 1, 0)
-    two = dot(two, first[:, HALF:], 1, 1)
+    one = product(site[:, :HALF], kept[:, :HALF], 1)
+    two = site[:, HALF:] - product(one, kept[:, HALF : 2 * HALF], 0)
+    two = product(two, first[:, HALF:], 1)
     out_ref[:, :here, :HALF] = (full_scale * one).reshape(peers, here, HALF)
     out_ref[:, :here, HALF:] = (full_scale * two).reshape(peers, here, HALF)
 
@@ -241,10 +308,10 @@
     scale = lax.rsqrt(squares * (1.0 / entries) + 1e-06)
     nxt = data_ref[:, here:, :].reshape(peers * STEP, breadth)
     nxt = jnp.where(column_ids < live_slot, nxt, 0.0)
-    one = dot(nxt[:, :HALF], kept[:, 2 * HALF : 3 * HALF], 1, 1) + dot(
-        nxt[:, HALF:], kept[:, 3 * HALF :], 1, 1
+    one = product(nxt[:, :HALF], kept[:, 2 * HALF : 3 * HALF], 1) + product(
+        nxt[:, HALF:], kept[:, 3 * HALF :], 1
     )
-    two = dot(nxt[:, HALF:], second[:, :HALF], 1, 1)
+    two = product(nxt[:, HALF:], second[:, :HALF], 1)
     out_ref[:, here:, :HALF] = (scale * one).reshape(peers, STEP, HALF)
     out_ref[:, here:, HALF:] = (scale * two).reshape(peers, STEP, HALF)
 
@@ -262,9 +329,13 @@
         gather_kernel,
         out_shape=jax.ShapeDtypeStruct((n_row, row_count + piece_columns, breadth), jnp.float32),
         in_specs=[HBM, HBM],
-        out_specs=VMEM,
-        scratch_shapes=[pltpu.SemaphoreType.DMA((2,))],
-        compiler_params=PARAMS,
+        out_specs=HBM,
+        scratch_shapes=[
+            pltpu.VMEM((n_row, row_count + piece_columns, breadth), jnp.float32),
+            pltpu.SemaphoreType.DMA((SHARES, 2)),
+            pltpu.SemaphoreType.DMA((SHARES,)),
+        ],
+        compiler_params=pltpu.CompilerParams(vmem_limit_bytes=60 * 1024 * 1024),
         name="gather",
     )(
         site_blocks.reshape(n_row, row_count, breadth),
@@ -312,6 +383,7 @@
             pltpu.VMEM((HALF, 2 * HALF), jnp.float32),
             pltpu.VMEM((HALF, 2 * HALF), jnp.float32),
             pltpu.VMEM((HALF, 4 * HALF), jnp.float32),
+            pltpu.VMEM((2 * STEP, 2 * HALF), jnp.float32),
         ],
         compiler_params=PARAMS,
         name="factor_apply",

time: 94.1 us -> 90.9 us (0.966)
  local copies, waits for them, and re-layouts: 6.07 us -> 4.05 us
  Pallas kernels: 15.7 us -> 14.6 us
    unnamed x13 -> x9, local copies, waits for them, and re-layouts: 3.3 us -> 1.32 us
    pallas_call x1, Pallas kernels: 11.1 us -> 9.15 us  [body(): pl.pallas_call(functools.partial(apply_kernel, entries), out_shape=jax.Sh...]
    pallas_call x1, Pallas kernels: 0.96 us -> 1.97 us  [body(): pl.pallas_call(gather_kernel, out_shape=jax.ShapeDtypeStruct((n_row, row_...]
where the time goes in v3:
time: 90.9 us; the launch traced here: 90.6 us
  blocking collectives  51.7 us (57%)
  Pallas kernels  14.6 us (16%)
  starting transfers between devices  9.43 us (10%)
  waiting for transfers between devices  8.14 us (9%)
  local copies, waits for them, and re-layouts  4.05 us (4%)
  other arithmetic  2.01 us (2%)
    all_to_all x2, blocking collectives, swap(): return lax.all_to_all(slots_of, both, 0, 0, tiled=True).reshape(x.shape)  33 us
    all_to_all x1, blocking collectives, body(): back = lax.all_to_all(result, 'row', 0, 0, tiled=True)  18.6 us
    all_to_all x1, starting transfers between devices, body(): data = lax.all_to_all(sent, 'row', 0, 0, tiled=True)  9.43 us
    pallas_call x1, Pallas kernels, body(): pl.pallas_call(functools.partial(apply_kernel, entries), out_shape=jax.Sh...  9.15 us
    all_to_all x1, waiting for transfers between devices, body(): data = lax.all_to_all(sent, 'row', 0, 0, tiled=True)  8.14 us
    another operation x1, other arithmetic, body(): meta = jnp.stack([rows_flat[me], join_flat[me], owner_flat[me], me])  2.01 us
    pallas_call x1, Pallas kernels, body(): pl.pallas_call(gather_kernel, out_shape=jax.ShapeDtypeStruct((n_row, row_...  1.97 us
    dynamic_slice x3, local copies, waits for them, and re-layouts, body(): meta = jnp.stack([rows_flat[me], join_flat[me], owner_flat[me], me])  1.85 us
  transfers between devices with their start and end apart: 1, of which 1 were waited for; matrix products, arithmetic and copies ran while one was open for 5% of the time, Pallas kernels for 0%

profile of v3, /device:TPU:1, one launch (start us, length us, event | category | flops | bytes accessed | tf_op | source)
XLA Modules:
  0.0 90.6 jit_solution(3754174909366020162)
XLA Ops:
  0.6 2.0 %gather.1 = f32[32,24,256]{2,1,0:T(8,128)} custom-call(f32[32,16,256]{2,1,0:T(8,128)} %bitcast.13, f32[32,8,256]{2,1,0:T(8,128)} %bitcast.14), custom_call_target="tpu_custom_call" | custom-call | tf_op jit(solution)/shard_map/gather/pallas_call | solution.py:328
  2.6 0.0 copy-start.1
  2.6 9.4 %all-to-all-start = ((f32[32,24,256]{2,1,0:T(8,128)}), f32[32,24,256]{2,1,0:T(8,128)S(1)}, u32[]{:S(2)}, u32[]{:S(2)}) async-start(f32[32,24,256]{2,1,0:T(8,128)} %gather.1), calls=%async_computation | async-start | bytes 1572864 | tf_op jit(solution)/shard_map/all_to_all | solution.py:357
  12.1 0.0 copy-done.1
  12.1 0.1 copy.22
  12.2 0.1 reshape_reshape.10.join_row
  12.3 0.0 copy-start.2
  12.3 0.1 reshape.51
  12.4 0.5 copy-done.2
  12.9 0.1 broadcast_in_dim.9
  13.0 0.1 reshape.52
  13.1 0.1 reshape_reshape.14.unused_two.owner_col
  13.2 0.1 reshape_reshape.13.unused_one.join_col
  13.3 0.0 copy-start.3
  13.3 0.7 copy-done.3
  13.9 0.1 broadcast_in_dim.10
  14.0 0.1 convert_element_type.6.rows_row
  14.1 0.7 dynamic_slice.10
  14.8 0.6 dynamic_slice.11
  15.3 0.1 broadcast_in_dim.8
  15.4 0.1 reshape.50
  15.5 0.6 dynamic_slice.9
  16.1 2.0 %pad_add_fusion.meta = s32[4]{0:T(128)S(1)} fusion(s32[1]{0:T(128)} %bitcast, s32[1]{0:T(128)} %dynamic_slice.11, s32[1]{0:T(128)} %dynamic_slice.10, s32[1]{0:T(128)} %dynamic_slice.9), kind=kLoop, calls=%fused_computation | loop fusion | flops 12 | bytes 32 | tf_op jit(solution)/shard_map/stack | solution.py:347
  18.2 8.1 %all-to-all-done.data_ref = f32[32,24,256]{2,1,0:T(8,128)S(1)} async-done(((f32[32,24,256]{2,1,0:T(8,128)}), f32[32,24,256]{2,1,0:T(8,128)S(1)}, u32[]{:S(2)}, u32[]{:S(2)}) %all-to-all-start) | async-done | bytes 786464 | tf_op jit(solution)/shard_map/all_to_all | solution.py:357
  26.3 0.0 copy-done
  26.3 1.5 %gram.1 = f32[640,128]{1,0:T(8,128)S(1)} custom-call(s32[4]{0:T(128)S(1)} %pad_add_fusion.meta, s32[32]{0:T(128)S(1)} %copy-done, s32[1,128]{1,0:T(1,128)S(1)} %reshape_reshape.10.join_row, f32[1,128]{1,0:T(1,128)S(1)} %convert_element_type.6.rows_row, s32[128,1]{1,0:T(8,128)S(1)} %reshape_reshape.13.unused_one.join_col, ...), custom_call_target="tpu_custom_call" | custom-call | tf_op jit(solution)/shard_map/gram/pallas_call | solution.py:358
  27.8 17.2 %all_to_all.20 = f32[128,1,640]{2,1,0:T(1,128)S(1)} all-to-all(f32[128,1,640]{2,1,0:T(1,128)S(1)} %bitcast.12), channel_id=1, replica_groups=mesh['grp'=4,'row'=32] {'grp','row'}, dimensions={0} | all-to-all | bytes 655360 | tf_op jit(solution)/shard_map/all_to_all | solution.py:355
  45.0 1.0 %combine.1 = f32[640,128]{1,0:T(8,128)S(1)} custom-call(s32[4]{0:T(128)S(1)} %pad_add_fusion.meta, s32[1,128]{1,0:T(1,128)S(1)} %reshape_reshape.10.join_row, s32[128,1]{1,0:T(8,128)S(1)} %reshape_reshape.13.unused_one.join_col, s32[128,1]{1,0:T(8,128)S(1)} %reshape_reshape.14.unused_two.owner_col, f32[640,128]{1,0:T(8,128)S(1)} %bitcast.9), custom_call_target="tpu_custom_call" | custom-call | tf_op jit(solution)/shard_map/combine/pallas_call | solution.py:367
  46.0 15.9 %all_to_all.21 = f32[128,1,640]{2,1,0:T(1,128)S(1)} all-to-all(f32[128,1,640]{2,1,0:T(1,128)S(1)} %bitcast.10), channel_id=1, replica_groups=mesh['grp'=4,'row'=32] {'grp','row'}, dimensions={0} | all-to-all | bytes 655360 | tf_op jit(solution)/shard_map/all_to_all | solution.py:355
  61.9 9.2 %factor_apply.1 = f32[32,24,256]{2,1,0:T(8,128)S(1)} custom-call(s32[4]{0:T(128)S(1)} %pad_add_fusion.meta, s32[32]{0:T(128)S(1)} %copy-done, s32[1,128]{1,0:T(1,128)S(1)} %reshape_reshape.10.join_row, f32[1,128]{1,0:T(1,128)S(1)} %convert_element_type.6.rows_row, f32[32,24,256]{2,1,0:T(8,128)S(1)} %all-to-all-done.data_ref, f32[640,128]{1,0:T(8,128)S(1)} %bitcast.11), custom_call_target="tpu_custom_call" | custom-call | tf_op jit(solution)/shard_map/factor_apply/pallas_call | solution.py:377
  71.1 18.6 %all_to_all.22.data_ref = f32[32,24,256]{2,1,0:T(8,128)S(1)} all-to-all(f32[32,24,256]{2,1,0:T(8,128)S(1)} %factor_apply.1), channel_id=1, replica_groups=mesh['grp'=4,'row'=32] {'row'}, dimensions={0} | all-to-all | bytes 1572864 | tf_op jit(solution)/shard_map/all_to_all | solution.py:391
  89.7 0.9 scatter.1
  (2 shorter events, 0.0 us)
Async XLA Ops:
  2.6 9.5 %copy-start.1 = (s32[32,4]{0,1:T(4,128)S(1)}, s32[32,4]{0,1:T(4,128)}, u32[]{:S(2)}) copy-start(s32[32,4]{0,1:T(4,128)} %param.9) | copy-start | bytes 1540
  2.6 23.7 %all-to-all-start = ((f32[32,24,256]{2,1,0:T(8,128)}), f32[32,24,256]{2,1,0:T(8,128)S(1)}, u32[]{:S(2)}, u32[]{:S(2)}) async-start(f32[32,24,256]{2,1,0:T(8,128)} %gather.1), calls=%async_computation | async-start | bytes 1572864 | tf_op jit(solution)/shard_map/all_to_all | solution.py:357
  12.3 0.7 copy-start.2
  13.3 0.7 copy-start.3
  16.1 10.1 %copy-start = (s32[32]{0:T(128)S(1)}, s32[32]{0:T(128)}, u32[]{:S(2)}) copy-start(s32[32]{0:T(128)} %column_lengths.3) | copy-start | bytes 388

commit v4 on v3

--- a/solution.py
+++ b/solution.py
@@ -13,7 +13,6 @@
 STEP = 8
 SLOT = 5
 WHEN = 4
-SHARES = 4
 HBM = pl.BlockSpec(memory_space=pltpu.HBM)
 PARAMS = pltpu.CompilerParams(vmem_limit_bytes=16 * 1024 * 1024)
 VMEM = pl.BlockSpec(memory_space=pltpu.VMEM)
@@ -26,33 +25,14 @@
     )
 
 
-def live_count(join_row, rows_row, column_lengths, sector):
-    joined = jnp.where(join_row[...] == sector, rows_row[...], 0.0)
-    joined = jnp.sum(joined, axis=1, keepdims=True)
-    return jnp.minimum(jnp.floor(joined * 0.5), column_lengths[sector].astype(jnp.float32))
-
-
-def gather_kernel(site_ref, next_ref, out_ref, held, in_sems, out_sems):
+def gather_kernel(site_ref, next_ref, out_ref, sems):
     here = site_ref.shape[1]
-    share = site_ref.shape[0] // SHARES
-    cuts = [pl.ds(i * share, share) for i in range(SHARES)]
-    arrivals = [
-        (
-            pltpu.make_async_copy(site_ref.at[cut], held.at[cut, :here, :], in_sems.at[i, 0]),
-            pltpu.make_async_copy(next_ref.at[cut], held.at[cut, here:, :], in_sems.at[i, 1]),
-        )
-        for i, cut in enumerate(cuts)
-    ]
-    leaves = [pltpu.make_async_copy(held.at[cut], out_ref.at[cut], out_sems.at[i]) for i, cut in enumerate(cuts)]
-    for pair in arrivals:
-        pair[0].start()
-        pair[1].start()
-    for pair, leave in zip(arrivals, leaves):
-        pair[0].wait()
-        pair[1].wait()
-        leave.start()
-    for leave in leaves:
-        leave.wait()
+    one = pltpu.make_async_copy(site_ref, out_ref.at[:, :here, :], sems.at[0])
+    two = pltpu.make_async_copy(next_ref, out_ref.at[:, here:, :], sems.at[1])
+    one.start()
+    two.start()
+    one.wait()
+    two.wait()
 
 
 def scatter_kernel(data_ref, site_ref, next_ref, sems):
@@ -69,33 +49,79 @@
     return pl.ds(index, HALF, stride=SLOT)
 
 
-def gram_kernel(meta, column_lengths, join_row, rows_row, unused_one, unused_two, data_ref, out_ref):
+def split(x):
+    high = x.astype(jnp.bfloat16).astype(jnp.float32)
+    rest = x - high
+    middle = rest.astype(jnp.bfloat16).astype(jnp.float32)
+    return high, middle, rest - middle
+
+
+def gram_kernel(
+    row_lengths,
+    column_lengths,
+    joining,
+    owner_slots,
+    rows_ref,
+    join_ref,
+    owner_ref,
+    data_ref,
+    out_ref,
+    meta_ref,
+    live_ref,
+    join_row,
+    join_col,
+    owner_col,
+):
+    states, sectors = join_ref.shape
+    n_row = lax.axis_size("row")
+    group, place = lax.axis_index("grp"), lax.axis_index("row")
+    left = group * (n_row // states) + place // states
+    meta_ref[0] = row_lengths[left]
+    meta_ref[1] = group * n_row + place
+    joins = join_ref[...]
+    for index, sector in enumerate((joining[place % states, left], owner_slots[left])):
+        joined = jnp.sum(jnp.where(joins == sector, rows_ref[...], 0), axis=0, keepdims=True)
+        joined = jnp.sum(joined.astype(jnp.float32), axis=1, keepdims=True)
+        live = jnp.minimum(jnp.floor(joined * 0.5), column_lengths[sector].astype(jnp.float32))
+        live_ref[index : index + 1, :] = jnp.broadcast_to(live, (1, HALF))
+    lefts = lax.broadcasted_iota(jnp.int32, (sectors, HALF), 0)
+    devices = lax.broadcasted_iota(jnp.int32, (sectors, HALF), 1)
+    expand = (devices // states == lefts).astype(jnp.float32)
+    by_state = dot(joins.astype(jnp.float32), expand, 1, 0)
+    state = lax.broadcasted_iota(jnp.int32, (states, HALF), 0)
+    device = lax.broadcasted_iota(jnp.int32, (states, HALF), 1)
+    row = jnp.sum(jnp.where(device % states == state, by_state, 0.0), axis=0, keepdims=True)
+    owners = dot(owner_ref[...].astype(jnp.float32), expand, 1, 0)
+    join_row[...] = row
+    sub = lax.broadcasted_iota(jnp.int32, (HALF, HALF), 0)
+    lane = lax.broadcasted_iota(jnp.int32, (HALF, HALF), 1)
+    join_col[...] = jnp.sum(jnp.where(sub == lane, row, 0.0), axis=1, keepdims=True)
+    owner_col[...] = jnp.sum(jnp.where(sub == lane, owners, 0.0), axis=1, keepdims=True)
     peers, depth, breadth = data_ref.shape
     here = depth - STEP
     site = data_ref[:, :here, :].reshape(peers * here, breadth)
     row_ids = lax.broadcasted_iota(jnp.int32, site.shape, 0)
-    site = jnp.where(row_ids < meta[0], site, 0.0)
+    site = jnp.where(row_ids < row_lengths[left], site, 0.0)
     nxt = data_ref[:, here:, :].reshape(peers * STEP, breadth)
-    live_slot = live_count(join_row, rows_row, column_lengths, meta[2])
+    live_slot = live
     column_ids = lax.broadcasted_iota(jnp.int32, (1, breadth), 1).astype(jnp.float32)
     nxt = jnp.where(column_ids < live_slot, nxt, 0.0)
     sub = lax.broadcasted_iota(jnp.int32, (HALF, HALF), 0)
     lane = lax.broadcasted_iota(jnp.int32, (HALF, HALF), 1)
     diagonals = []
     for start, block in ((0, site), (2, nxt)):
-        top = dot(block[:, :HALF], block, 0, 0)
-        low = dot(block[:, HALF:], block[:, HALF:], 0, 0)
+        high, middle, low = (part.astype(jnp.bfloat16) for part in split(block))
+        dims = (((0,), (0,)), ((), ()))
+        wide = lax.dot_general(high, middle, dims, preferred_element_type=jnp.float32)
+        wide = wide + lax.dot_general(high, low, dims, preferred_element_type=jnp.float32)
+        square = lax.dot_general(high, high, dims, preferred_element_type=jnp.float32)
+        square = square + lax.dot_general(middle, middle, dims, preferred_element_type=jnp.float32)
+        square = square + (wide + wide.T)
+        top, low = square[:HALF], square[HALF:, HALF:]
         out_ref[slot_rows(start), :] = jnp.where(sub <= lane, top[:, :HALF], low)
         out_ref[slot_rows(start + 1), :] = top[:, HALF:]
         diagonals.append(jnp.sum(jnp.where(sub == lane, low, 0.0), axis=1, keepdims=True))
     out_ref[slot_rows(4), :] = jnp.where(lane < HALF // 2, diagonals[0], diagonals[1])
-
-
-def split(x):
-    high = x.astype(jnp.bfloat16).astype(jnp.float32)
-    rest = x - high
-    middle = rest.astype(jnp.bfloat16).astype(jnp.float32)
-    return high, middle, rest - middle
 
 
 def combine_kernel(meta, join_row, join_col, owner_col, piece_ref, out_ref):
@@ -117,7 +143,7 @@
     out_ref[slot_rows(2), :] = slot_part[:, packed]
     out_ref[slot_rows(3), :] = slot_part[:, cross]
     lane = lax.broadcasted_iota(jnp.int32, (1, HALF), 1)
-    norm = jnp.where(lane == meta[3], 1.0, 2.0) * slot_part[:, packed] * piece_ref[slot_rows(2), :]
+    norm = jnp.where(lane == meta[1], 1.0, 2.0) * slot_part[:, packed] * piece_ref[slot_rows(2), :]
     norm = norm + 2.0 * slot_part[:, cross] * piece_ref[slot_rows(3), :]
     moment = jnp.where(lane == HALF - 1, pltpu.roll(slot_part[:, diagonal], HALF // 2, 1), 0.0)
     norm = norm + moment * piece_ref[slot_rows(4), :]
@@ -242,12 +268,12 @@
 
 
 def apply_kernel(
-    entries, meta, column_lengths, join_row, rows_row, data_ref, gram_ref, out_ref, first, second, kept, turn
+    entries, meta, live_ref, data_ref, gram_ref, out_ref, first, second, kept, turn
 ):
     peers, depth, breadth = data_ref.shape
     here = depth - STEP
-    live_pair = live_count(join_row, rows_row, column_lengths, meta[1])
-    live_slot = live_count(join_row, rows_row, column_lengths, meta[2])
+    live_pair = live_ref[:1, :1]
+    live_slot = live_ref[1:2, :1]
     sub = lax.broadcasted_iota(jnp.int32, (HALF, HALF), 0)
     lane = lax.broadcasted_iota(jnp.int32, (HALF, HALF), 1)
     eye = jnp.where(sub == lane, 1.0, 0.0)
@@ -290,7 +316,7 @@
 
         return carry
 
-    lax.fori_loop(0, 2, half, 0)
+    lax.fori_loop(0, 2, half, 0, unroll=True)
 
     column_ids = lax.broadcasted_iota(jnp.int32, (1, breadth), 1).astype(jnp.float32)
     site = data_ref[:, :here, :].reshape(peers * here, breadth)
@@ -322,47 +348,54 @@
     n_row = lax.axis_size("row")
     n_all = n_row * lax.axis_size("grp")
     both = ("grp", "row")
-    me = lax.axis_index("grp") * n_row + lax.axis_index("row")
     quarters = n_row // slots
     piece_columns = local_columns // quarters
     sent = pl.pallas_call(
         gather_kernel,
         out_shape=jax.ShapeDtypeStruct((n_row, row_count + piece_columns, breadth), jnp.float32),
         in_specs=[HBM, HBM],
-        out_specs=HBM,
-        scratch_shapes=[
-            pltpu.VMEM((n_row, row_count + piece_columns, breadth), jnp.float32),
-            pltpu.SemaphoreType.DMA((SHARES, 2)),
-            pltpu.SemaphoreType.DMA((SHARES,)),
-        ],
-        compiler_params=pltpu.CompilerParams(vmem_limit_bytes=60 * 1024 * 1024),
+        out_specs=VMEM,
+        scratch_shapes=[pltpu.SemaphoreType.DMA((2,))],
+        compiler_params=PARAMS,
         name="gather",
     )(
-        site_blocks.reshape(n_row, row_count, breadth),
-        next_blocks.reshape(n_row, piece_columns, breadth),
+        pltpu.with_memory_space_constraint(
+            site_blocks.reshape(n_row, row_count, breadth), pltpu.HBM
+        ),
+        pltpu.with_memory_space_constraint(
+            next_blocks.reshape(n_row, piece_columns, breadth), pltpu.HBM
+        ),
     )
-    join_flat = joining.reshape(-1)
-    owner_flat = jnp.repeat(owner_slots, quarters)
-    rows_flat = jnp.repeat(row_lengths, states)
-    meta = jnp.stack([rows_flat[me], join_flat[me], owner_flat[me], me])
-    join_row = join_flat.reshape(1, n_all)
-    join_col = join_flat.reshape(n_all, 1)
-    owner_col = owner_flat.reshape(n_all, 1)
-    rows_row = rows_flat.reshape(1, n_all).astype(jnp.float32)
 
     def swap(x):
         slots_of = x.reshape(n_all, 1, SLOT * HALF)
         return lax.all_to_all(slots_of, both, 0, 0, tiled=True).reshape(x.shape)
 
     data = lax.all_to_all(sent, "row", 0, 0, tiled=True)
-    gram = pl.pallas_call(
+    gram, meta, live, join_row, join_col, owner_col = pl.pallas_call(
         gram_kernel,
-        out_shape=jax.ShapeDtypeStruct((n_all * SLOT, HALF), jnp.float32),
-        in_specs=[SMEM, SMEM, VMEM, VMEM, VMEM, VMEM, VMEM],
-        out_specs=VMEM,
+        out_shape=(
+            jax.ShapeDtypeStruct((n_all * SLOT, HALF), jnp.float32),
+            jax.ShapeDtypeStruct((2,), jnp.int32),
+            jax.ShapeDtypeStruct((2, HALF), jnp.float32),
+            jax.ShapeDtypeStruct((1, n_all), jnp.float32),
+            jax.ShapeDtypeStruct((n_all, 1), jnp.float32),
+            jax.ShapeDtypeStruct((n_all, 1), jnp.float32),
+        ),
+        in_specs=[SMEM, SMEM, SMEM, SMEM, VMEM, VMEM, VMEM, VMEM],
+        out_specs=(VMEM, SMEM, VMEM, VMEM, VMEM, VMEM),
         compiler_params=PARAMS,
         name="gram",
-    )(meta, column_lengths, join_row, rows_row, join_col, owner_col, data)
+    )(
+        row_lengths,
+        column_lengths,
+        joining.T,
+        owner_slots,
+        row_lengths.reshape(1, -1),
+        joining.T,
+        owner_slots.reshape(1, -1),
+        data,
+    )
     pieces = swap(gram)
     rows = pl.pallas_call(
         combine_kernel,
@@ -377,7 +410,7 @@
     result = pl.pallas_call(
         functools.partial(apply_kernel, entries),
         out_shape=jax.ShapeDtypeStruct(sent.shape, jnp.float32),
-        in_specs=[SMEM, SMEM, VMEM, VMEM, VMEM, VMEM],
+        in_specs=[SMEM, VMEM, VMEM, VMEM],
         out_specs=VMEM,
         scratch_shapes=[
             pltpu.VMEM((HALF, 2 * HALF), jnp.float32),
@@ -387,7 +420,7 @@
         ],
         compiler_params=PARAMS,
         name="factor_apply",
-    )(meta, column_lengths, join_row, rows_row, data, grams)
+    )(meta, live, data, grams)
     back = lax.all_to_all(result, "row", 0, 0, tiled=True)
     canonical, next_site = pl.pallas_call(
         scatter_kernel,

time: 90.9 us -> 90.4 us (level)
  blocking collectives: 51.7 us -> 75.1 us
  starting transfers between devices: 9.43 us -> 0 us
  waiting for transfers between devices: 8.14 us -> 0 us
  local copies, waits for them, and re-layouts: 4.05 us -> 0.7 us
  other arithmetic: 2.01 us -> 0 us
  Pallas kernels: 14.6 us -> 13.6 us
    all_to_all x0 -> x1, blocking collectives: none -> 23.5 us  [body(): data = lax.all_to_all(sent, 'row', 0, 0, tiled=True)]
    all_to_all x1 -> x0, starting transfers between devices: 9.43 us -> none  [body(): data = lax.all_to_all(sent, 'row', 0, 0, tiled=True)]
    all_to_all x1 -> x0, waiting for transfers between devices: 8.14 us -> none  [body(): data = lax.all_to_all(sent, 'row', 0, 0, tiled=True)]
    another operation x1 -> x0, other arithmetic: 2.01 us -> none  [body(): meta = jnp.stack([rows_flat[me], join_flat[me], owner_flat[me], me])]
    dynamic_slice x3 -> x0, local copies, waits for them, and re-layouts: 1.85 us -> none  [body(): meta = jnp.stack([rows_flat[me], join_flat[me], owner_flat[me], me])]
  transfers between devices with their start and end apart: 1 -> 0, of which waited for: 1 -> 0; matrix products, arithmetic and copies ran while one was open for 5% -> 0% of each run, Pallas kernels for 0% -> 0%
where the time goes in v4:
time: 90.4 us; the launch traced here: 90.1 us
  blocking collectives  75.1 us (83%)
  Pallas kernels  13.6 us (15%)
    all_to_all x2, blocking collectives, swap(): return lax.all_to_all(slots_of, both, 0, 0, tiled=True).reshape(x.shape)  33 us
    all_to_all x1, blocking collectives, body(): data = lax.all_to_all(sent, 'row', 0, 0, tiled=True)  23.5 us
    all_to_all x1, blocking collectives, body(): back = lax.all_to_all(result, 'row', 0, 0, tiled=True)  18.6 us
    pallas_call x1, Pallas kernels, body(): pl.pallas_call(functools.partial(apply_kernel, entries), out_shape=jax.Sh...  8.95 us

profile of v4, /device:TPU:1, one launch (start us, length us, event | category | flops | bytes accessed | tf_op | source)
XLA Modules:
  0.0 90.1 jit_solution(5347012374864081032)
XLA Ops:
  0.6 1.1 %gather.1 = f32[32,24,256]{2,1,0:T(8,128)S(1)} custom-call(f32[32,16,256]{2,1,0:T(8,128)} %bitcast.19, f32[32,8,256]{2,1,0:T(8,128)} %bitcast.20), custom_call_target="tpu_custom_call" | custom-call | tf_op jit(solution)/shard_map/gather/pallas_call | solution.py:353
  1.8 23.5 %all_to_all.20.data_ref = f32[32,24,256]{2,1,0:T(8,128)S(1)} all-to-all(f32[32,24,256]{2,1,0:T(8,128)S(1)} %gather.1), channel_id=1, replica_groups=mesh['grp'=4,'row'=32] {'row'}, dimensions={0} | all-to-all | bytes 1572864 | tf_op jit(solution)/shard_map/all_to_all | solution.py:374
  25.2 0.0 copy-start
  25.2 0.0 copy-start.1
  25.2 0.0 copy-start.2
  25.2 0.0 copy-start.3
  25.2 0.7 copy-done
  25.9 0.0 copy-done.1
  25.9 0.0 copy-done.2
  25.9 0.0 copy-done.3
  25.9 1.6 %gram.1 = (f32[640,128]{1,0:T(8,128)S(1)}, s32[2]{0:T(128)S(1)}, f32[2,128]{1,0:T(2,128)S(1)}, f32[1,128]{1,0:T(1,128)S(1)}, f32[128,1]{1,0:T(8,128)S(1)}, /*index=5*/f32[128,1]{1,0:T(8,128)S(1)}) custom-call(s32[32]{0:T(128)S(1)} %copy-done.1, s32[32]{0:T(128)S(1)} %copy-done.3, s32[4,32]{1,0:T(4,128)S(1)} %bitcast.15, s32[32]{0:T(128)S(1)} %copy-done.2, ...), custom_call_target="tpu_custom_call" | custom-call | tf_op jit(solution)/shard_map/gram/pallas_call | solution.py:375
  27.6 17.2 %all_to_all.21 = f32[128,1,640]{2,1,0:T(1,128)S(1)} all-to-all(f32[128,1,640]{2,1,0:T(1,128)S(1)} %bitcast.14), channel_id=1, replica_groups=mesh['grp'=4,'row'=32] {'grp','row'}, dimensions={0} | all-to-all | bytes 655360 | tf_op jit(solution)/shard_map/all_to_all | solution.py:372
  44.7 1.0 %combine.1 = f32[640,128]{1,0:T(8,128)S(1)} custom-call(s32[2]{0:T(128)S(1)} %get-tuple-element.10.meta, f32[1,128]{1,0:T(1,128)S(1)} %get-tuple-element.12.join_row, f32[128,1]{1,0:T(8,128)S(1)} %get-tuple-element.13.join_col, f32[128,1]{1,0:T(8,128)S(1)} %get-tuple-element.14.owner_col, f32[640,128]{1,0:T(8,128)S(1)} %bitcast.11), custom_call_target="tpu_custom_call" | custom-call | tf_op jit(solution)/shard_map/combine/pallas_call | solution.py:400
  45.8 15.9 %all_to_all.22 = f32[128,1,640]{2,1,0:T(1,128)S(1)} all-to-all(f32[128,1,640]{2,1,0:T(1,128)S(1)} %bitcast.12), channel_id=1, replica_groups=mesh['grp'=4,'row'=32] {'grp','row'}, dimensions={0} | all-to-all | bytes 655360 | tf_op jit(solution)/shard_map/all_to_all | solution.py:372
  61.6 8.9 %factor_apply.1 = f32[32,24,256]{2,1,0:T(8,128)S(1)} custom-call(s32[2]{0:T(128)S(1)} %get-tuple-element.10.meta, f32[2,128]{1,0:T(2,128)S(1)} %get-tuple-element.11.live_ref, f32[32,24,256]{2,1,0:T(8,128)S(1)} %all_to_all.20.data_ref, f32[640,128]{1,0:T(8,128)S(1)} %bitcast.13), custom_call_target="tpu_custom_call" | custom-call | tf_op jit(solution)/shard_map/factor_apply/pallas_call | solution.py:410
  70.6 18.6 %all_to_all.23.data_ref = f32[32,24,256]{2,1,0:T(8,128)S(1)} all-to-all(f32[32,24,256]{2,1,0:T(8,128)S(1)} %factor_apply.1), channel_id=1, replica_groups=mesh['grp'=4,'row'=32] {'row'}, dimensions={0} | all-to-all | bytes 1572864 | tf_op jit(solution)/shard_map/all_to_all | solution.py:424
  89.2 0.9 scatter.1
Async XLA Ops:
  25.2 0.7 copy-start
  25.2 0.7 copy-start.1
  25.2 0.7 copy-start.2
  25.2 0.7 copy-start.3

commit v5 on v4

--- a/solution.py
+++ b/solution.py
@@ -25,14 +25,19 @@
     )
 
 
-def gather_kernel(site_ref, next_ref, out_ref, sems):
+def gather_kernel(site_ref, next_ref, *refs):
+    tables, out_ref, held, sems = refs[:4], refs[4], refs[5:9], refs[9]
     here = site_ref.shape[1]
-    one = pltpu.make_async_copy(site_ref, out_ref.at[:, :here, :], sems.at[0])
-    two = pltpu.make_async_copy(next_ref, out_ref.at[:, here:, :], sems.at[1])
-    one.start()
-    two.start()
-    one.wait()
-    two.wait()
+    copies = [
+        pltpu.make_async_copy(site_ref, out_ref.at[:, :here, :], sems.at[0]),
+        pltpu.make_async_copy(next_ref, out_ref.at[:, here:, :], sems.at[1]),
+    ]
+    for i in range(4):
+        copies.append(pltpu.make_async_copy(tables[i], held[i], sems.at[2 + i]))
+    for copy in copies:
+        copy.start()
+    for copy in copies:
+        copy.wait()
 
 
 def scatter_kernel(data_ref, site_ref, next_ref, sems):
@@ -76,13 +81,13 @@
     n_row = lax.axis_size("row")
     group, place = lax.axis_index("grp"), lax.axis_index("row")
     left = group * (n_row // states) + place // states
-    meta_ref[0] = row_lengths[left]
+    meta_ref[0] = row_lengths[0, left]
     meta_ref[1] = group * n_row + place
     joins = join_ref[...]
-    for index, sector in enumerate((joining[place % states, left], owner_slots[left])):
+    for index, sector in enumerate((joining[place % states, left], owner_slots[0, left])):
         joined = jnp.sum(jnp.where(joins == sector, rows_ref[...], 0), axis=0, keepdims=True)
         joined = jnp.sum(joined.astype(jnp.float32), axis=1, keepdims=True)
-        live = jnp.minimum(jnp.floor(joined * 0.5), column_lengths[sector].astype(jnp.float32))
+        live = jnp.minimum(jnp.floor(joined * 0.5), column_lengths[0, sector].astype(jnp.float32))
         live_ref[index : index + 1, :] = jnp.broadcast_to(live, (1, HALF))
     lefts = lax.broadcasted_iota(jnp.int32, (sectors, HALF), 0)
     devices = lax.broadcasted_iota(jnp.int32, (sectors, HALF), 1)
@@ -101,7 +106,7 @@
     here = depth - STEP
     site = data_ref[:, :here, :].reshape(peers * here, breadth)
     row_ids = lax.broadcasted_iota(jnp.int32, site.shape, 0)
-    site = jnp.where(row_ids < row_lengths[left], site, 0.0)
+    site = jnp.where(row_ids < row_lengths[0, left], site, 0.0)
     nxt = data_ref[:, here:, :].reshape(peers * STEP, breadth)
     live_slot = live
     column_ids = lax.broadcasted_iota(jnp.int32, (1, breadth), 1).astype(jnp.float32)
@@ -350,22 +355,28 @@
     both = ("grp", "row")
     quarters = n_row // slots
     piece_columns = local_columns // quarters
-    sent = pl.pallas_call(
+    tables = (
+        row_lengths.reshape(1, -1),
+        column_lengths.reshape(1, -1),
+        joining.T,
+        owner_slots.reshape(1, -1),
+    )
+    arrays = (
+        site_blocks.reshape(n_row, row_count, breadth),
+        next_blocks.reshape(n_row, piece_columns, breadth),
+    ) + tables
+    sent, rows_line, columns_line, joins, owner_line = pl.pallas_call(
         gather_kernel,
-        out_shape=jax.ShapeDtypeStruct((n_row, row_count + piece_columns, breadth), jnp.float32),
-        in_specs=[HBM, HBM],
-        out_specs=VMEM,
-        scratch_shapes=[pltpu.SemaphoreType.DMA((2,))],
+        out_shape=(
+            jax.ShapeDtypeStruct((n_row, row_count + piece_columns, breadth), jnp.float32),
+        )
+        + tuple(jax.ShapeDtypeStruct(t.shape, t.dtype) for t in tables),
+        in_specs=[HBM] * 6,
+        out_specs=(VMEM,) * 5,
+        scratch_shapes=[pltpu.SemaphoreType.DMA((6,))],
         compiler_params=PARAMS,
         name="gather",
-    )(
-        pltpu.with_memory_space_constraint(
-            site_blocks.reshape(n_row, row_count, breadth), pltpu.HBM
-        ),
-        pltpu.with_memory_space_constraint(
-            next_blocks.reshape(n_row, piece_columns, breadth), pltpu.HBM
-        ),
-    )
+    )(*(pltpu.with_memory_space_constraint(x, pltpu.HBM) for x in arrays))
 
     def swap(x):
         slots_of = x.reshape(n_all, 1, SLOT * HALF)
@@ -387,13 +398,13 @@
         compiler_params=PARAMS,
         name="gram",
     )(
-        row_lengths,
-        column_lengths,
-        joining.T,
-        owner_slots,
-        row_lengths.reshape(1, -1),
-        joining.T,
-        owner_slots.reshape(1, -1),
+        rows_line,
+        columns_line,
+        joins,
+        owner_line,
+        rows_line,
+        joins,
+        owner_line,
         data,
     )
     pieces = swap(gram)

time: 90.4 us -> 89.7 us (level)
  no operation moved by 1% of the time
where the time goes in v5:
time: 89.7 us; the launch traced here: 89.5 us
  blocking collectives  75.1 us (84%)
  Pallas kernels  13.7 us (15%)
    all_to_all x2, blocking collectives, swap(): return lax.all_to_all(slots_of, both, 0, 0, tiled=True).reshape(x.shape)  33 us
    all_to_all x1, blocking collectives, body(): data = lax.all_to_all(sent, 'row', 0, 0, tiled=True)  23.5 us
    all_to_all x1, blocking collectives, body(): back = lax.all_to_all(result, 'row', 0, 0, tiled=True)  18.6 us
    pallas_call x1, Pallas kernels, body(): pl.pallas_call(functools.partial(apply_kernel, entries), out_shape=jax.Sh...  8.95 us

profile of v5, /device:TPU:1, one launch (start us, length us, event | category | flops | bytes accessed | tf_op | source)
XLA Modules:
  0.0 89.5 jit_solution(919277243632604419)
XLA Ops:
  0.6 1.2 %gather.1 = (f32[32,24,256]{2,1,0:T(8,128)S(1)}, s32[1,32]{1,0:T(1,128)S(1)}, s32[1,32]{1,0:T(1,128)S(1)}, s32[4,32]{1,0:T(4,128)S(1)}, s32[1,32]{1,0:T(1,128)S(1)}) custom-call(f32[32,16,256]{2,1,0:T(8,128)} %bitcast.16, f32[32,8,256]{2,1,0:T(8,128)} %bitcast.17, s32[1,32]{1,0:T(1,128)} %bitcast.19, s32[1,32]{1,0:T(1,128)} %bitcast.20, s32[4,32]{1,0:T(4,128)} %bitcast.18, ...), custom_call_target="tpu_custom_call" | custom-call | tf_op jit(solution)/shard_map/gather/pallas_call | solution.py:368
  1.8 23.5 %all_to_all.20.data_ref = f32[32,24,256]{2,1,0:T(8,128)S(1)} all-to-all(f32[32,24,256]{2,1,0:T(8,128)S(1)} %get-tuple-element.19), channel_id=1, replica_groups=mesh['grp'=4,'row'=32] {'row'}, dimensions={0} | all-to-all | bytes 1572864 | tf_op jit(solution)/shard_map/all_to_all | solution.py:385
  25.3 1.6 %gram.1 = (f32[640,128]{1,0:T(8,128)S(1)}, s32[2]{0:T(128)S(1)}, f32[2,128]{1,0:T(2,128)S(1)}, f32[1,128]{1,0:T(1,128)S(1)}, f32[128,1]{1,0:T(8,128)S(1)}, /*index=5*/f32[128,1]{1,0:T(8,128)S(1)}) custom-call(s32[1,32]{1,0:T(1,128)S(1)} %get-tuple-element.15.row_lengths.rows_ref, s32[1,32]{1,0:T(1,128)S(1)} %get-tuple-element.16.column_lengths, ...), custom_call_target="tpu_custom_call" | custom-call | tf_op jit(solution)/shard_map/gram/pallas_call | solution.py:386
  26.9 17.2 %all_to_all.21 = f32[128,1,640]{2,1,0:T(1,128)S(1)} all-to-all(f32[128,1,640]{2,1,0:T(1,128)S(1)} %bitcast.15), channel_id=1, replica_groups=mesh['grp'=4,'row'=32] {'grp','row'}, dimensions={0} | all-to-all | bytes 655360 | tf_op jit(solution)/shard_map/all_to_all | solution.py:383
  44.1 1.0 %combine.1 = f32[640,128]{1,0:T(8,128)S(1)} custom-call(s32[2]{0:T(128)S(1)} %get-tuple-element.20.meta, f32[1,128]{1,0:T(1,128)S(1)} %get-tuple-element.22.join_row, f32[128,1]{1,0:T(8,128)S(1)} %get-tuple-element.23.join_col, f32[128,1]{1,0:T(8,128)S(1)} %get-tuple-element.24.owner_col, f32[640,128]{1,0:T(8,128)S(1)} %bitcast.12), custom_call_target="tpu_custom_call" | custom-call | tf_op jit(solution)/shard_map/combine/pallas_call | solution.py:411
  45.1 15.9 %all_to_all.22 = f32[128,1,640]{2,1,0:T(1,128)S(1)} all-to-all(f32[128,1,640]{2,1,0:T(1,128)S(1)} %bitcast.13), channel_id=1, replica_groups=mesh['grp'=4,'row'=32] {'grp','row'}, dimensions={0} | all-to-all | bytes 655360 | tf_op jit(solution)/shard_map/all_to_all | solution.py:383
  61.0 8.9 %factor_apply.1 = f32[32,24,256]{2,1,0:T(8,128)S(1)} custom-call(s32[2]{0:T(128)S(1)} %get-tuple-element.20.meta, f32[2,128]{1,0:T(2,128)S(1)} %get-tuple-element.21.live_ref, f32[32,24,256]{2,1,0:T(8,128)S(1)} %all_to_all.20.data_ref, f32[640,128]{1,0:T(8,128)S(1)} %bitcast.14), custom_call_target="tpu_custom_call" | custom-call | tf_op jit(solution)/shard_map/factor_apply/pallas_call | solution.py:421
  69.9 18.6 %all_to_all.23.data_ref = f32[32,24,256]{2,1,0:T(8,128)S(1)} all-to-all(f32[32,24,256]{2,1,0:T(8,128)S(1)} %factor_apply.1), channel_id=1, replica_groups=mesh['grp'=4,'row'=32] {'row'}, dimensions={0} | all-to-all | bytes 1572864 | tf_op jit(solution)/shard_map/all_to_all | solution.py:435
  88.6 0.9 scatter.1

commit v6 on v5

--- a/solution.py
+++ b/solution.py
@@ -306,7 +306,7 @@
         @pl.when(index == 0)
         def _():
             pair_turn = first[:, HALF:]
-            pair_cross = dot(pair_turn, masked(1, live_pair, 0, HALF), 1, 0)
+            pair_cross = product(pair_turn, masked(1, live_pair, 0, HALF), 0)
             slot_cross = second[:, HALF:]
             kept[:, :HALF] = pair_turn
             kept[:, HALF : 2 * HALF] = pair_cross

time: 89.7 us -> 89.7 us (level)
  no operation moved by 1% of the time
where the time goes in v6:
time: 89.7 us; the launch traced here: 89.4 us
  blocking collectives  75.1 us (84%)
  Pallas kernels  13.6 us (15%)
    all_to_all x2, blocking collectives, swap(): return lax.all_to_all(slots_of, both, 0, 0, tiled=True).reshape(x.shape)  33 us
    all_to_all x1, blocking collectives, body(): data = lax.all_to_all(sent, 'row', 0, 0, tiled=True)  23.5 us
    all_to_all x1, blocking collectives, body(): back = lax.all_to_all(result, 'row', 0, 0, tiled=True)  18.6 us
    pallas_call x1, Pallas kernels, body(): pl.pallas_call(functools.partial(apply_kernel, entries), out_shape=jax.Sh...  8.9 us

profile of v6, /device:TPU:1, one launch (start us, length us, event | category | flops | bytes accessed | tf_op | source)
XLA Modules:
  0.0 89.4 jit_solution(837362362454568490)
XLA Ops:
  0.6 1.2 %gather.1 = (f32[32,24,256]{2,1,0:T(8,128)S(1)}, s32[1,32]{1,0:T(1,128)S(1)}, s32[1,32]{1,0:T(1,128)S(1)}, s32[4,32]{1,0:T(4,128)S(1)}, s32[1,32]{1,0:T(1,128)S(1)}) custom-call(f32[32,16,256]{2,1,0:T(8,128)} %bitcast.16, f32[32,8,256]{2,1,0:T(8,128)} %bitcast.17, s32[1,32]{1,0:T(1,128)} %bitcast.19, s32[1,32]{1,0:T(1,128)} %bitcast.20, s32[4,32]{1,0:T(4,128)} %bitcast.18, ...), custom_call_target="tpu_custom_call" | custom-call | tf_op jit(solution)/shard_map/gather/pallas_call | solution.py:368
  1.8 23.5 %all_to_all.20.data_ref = f32[32,24,256]{2,1,0:T(8,128)S(1)} all-to-all(f32[32,24,256]{2,1,0:T(8,128)S(1)} %get-tuple-element.19), channel_id=1, replica_groups=mesh['grp'=4,'row'=32] {'row'}, dimensions={0} | all-to-all | bytes 1572864 | tf_op jit(solution)/shard_map/all_to_all | solution.py:385
  25.3 1.6 %gram.1 = (f32[640,128]{1,0:T(8,128)S(1)}, s32[2]{0:T(128)S(1)}, f32[2,128]{1,0:T(2,128)S(1)}, f32[1,128]{1,0:T(1,128)S(1)}, f32[128,1]{1,0:T(8,128)S(1)}, /*index=5*/f32[128,1]{1,0:T(8,128)S(1)}) custom-call(s32[1,32]{1,0:T(1,128)S(1)} %get-tuple-element.15.row_lengths.rows_ref, s32[1,32]{1,0:T(1,128)S(1)} %get-tuple-element.16.column_lengths, ...), custom_call_target="tpu_custom_call" | custom-call | tf_op jit(solution)/shard_map/gram/pallas_call | solution.py:386
  26.9 17.2 %all_to_all.21 = f32[128,1,640]{2,1,0:T(1,128)S(1)} all-to-all(f32[128,1,640]{2,1,0:T(1,128)S(1)} %bitcast.15), channel_id=1, replica_groups=mesh['grp'=4,'row'=32] {'grp','row'}, dimensions={0} | all-to-all | bytes 655360 | tf_op jit(solution)/shard_map/all_to_all | solution.py:383
  44.1 1.0 %combine.1 = f32[640,128]{1,0:T(8,128)S(1)} custom-call(s32[2]{0:T(128)S(1)} %get-tuple-element.20.meta, f32[1,128]{1,0:T(1,128)S(1)} %get-tuple-element.22.join_row, f32[128,1]{1,0:T(8,128)S(1)} %get-tuple-element.23.join_col, f32[128,1]{1,0:T(8,128)S(1)} %get-tuple-element.24.owner_col, f32[640,128]{1,0:T(8,128)S(1)} %bitcast.12), custom_call_target="tpu_custom_call" | custom-call | tf_op jit(solution)/shard_map/combine/pallas_call | solution.py:411
  45.1 15.9 %all_to_all.22 = f32[128,1,640]{2,1,0:T(1,128)S(1)} all-to-all(f32[128,1,640]{2,1,0:T(1,128)S(1)} %bitcast.13), channel_id=1, replica_groups=mesh['grp'=4,'row'=32] {'grp','row'}, dimensions={0} | all-to-all | bytes 655360 | tf_op jit(solution)/shard_map/all_to_all | solution.py:383
  61.0 8.9 %factor_apply.1 = f32[32,24,256]{2,1,0:T(8,128)S(1)} custom-call(s32[2]{0:T(128)S(1)} %get-tuple-element.20.meta, f32[2,128]{1,0:T(2,128)S(1)} %get-tuple-element.21.live_ref, f32[32,24,256]{2,1,0:T(8,128)S(1)} %all_to_all.20.data_ref, f32[640,128]{1,0:T(8,128)S(1)} %bitcast.14), custom_call_target="tpu_custom_call" | custom-call | tf_op jit(solution)/shard_map/factor_apply/pallas_call | solution.py:421
  69.9 18.6 %all_to_all.23.data_ref = f32[32,24,256]{2,1,0:T(8,128)S(1)} all-to-all(f32[32,24,256]{2,1,0:T(8,128)S(1)} %factor_apply.1), channel_id=1, replica_groups=mesh['grp'=4,'row'=32] {'row'}, dimensions={0} | all-to-all | bytes 1572864 | tf_op jit(solution)/shard_map/all_to_all | solution.py:435
  88.5 0.9 scatter.1
